TPU v7x, 512 devices: a whole 4x8x8 slice. The times are simulated.
512 devices in a mesh: win: 8 (over z_hi, core), slab: 64 (over z_lo, x, y).
Axes of the slice: x: 4, y: 8, z: 8 (z_hi: 4, z_lo: 2; z = z_hi * 2 + z_lo), core: 2. Of those that a mesh axis runs over, the one named last changes fastest.
Arguments:
- states: float32 [8, 6, 128, 64, 256], P('win', None, 'slab'), may hold values from -6 to 6
- load_shape: bfloat16 [3, 128, 64, 256], P(None, 'slab'), may hold values from -6 to 6
- zone_ids: int32 [128, 64, 256], P('slab'), may hold values from 0 to 7
- zone_shear: float32 [8], replicated, may hold values from 0.3 to 1.2
- zone_lame: float32 [8], replicated, may hold values from 0.3 to 1.5
- amp_table: float32 [16], replicated, may hold values from 0.5 to 2
- cycle_index: int32 [16], replicated, may hold values from 0 to 15, each once
Outputs:
- new_ends: float32 [8, 6, 128, 64, 256], P('win', None, 'slab')
Inputs may be any that keep to these rules, and one draw needn't show every extreme that they name: cycle_index holds each of 0 to 15 once.
All inputs are finite; a program needn't handle non-finite values.
Results may differ from a plain program's by a relative error of at most 0.0003.
Values sent between devices are 32-bit elements; how exact they have to be, the bound alone decides.
A program may use at most 64 MiB of HBM per device.

v0:
```python
import jax
import jax.numpy as jnp
from jax import lax
from jax.sharding import PartitionSpec as P

FINE = 4
COARSE = 2


DT_FINE = 0.18
DT_COARSE = 0.36
FACE_WEIGHT = 14.0 / 30.0
EDGE_WEIGHT = 3.0 / 30.0
CORNER_WEIGHT = 1.0 / 30.0


def padded_2(block, sides, width):
    for axis, dim in sides:
        count = lax.axis_size(axis)
        forward = [(i, i + 1) for i in range(count - 1)]
        backward = [(target, source) for source, target in forward]
        low = lax.ppermute(
            lax.slice_in_dim(block, block.shape[dim] - width, None, axis=dim), axis, forward
        )
        high = lax.ppermute(lax.slice_in_dim(block, 0, width, axis=dim), axis, backward)
        block = jnp.concatenate([low, block, high], axis=dim)
    return block


def passed_along(block, axis, distance):
    devices = range(lax.axis_size(axis))
    route = [(i - distance, i) for i in devices if i - distance in devices]
    return lax.ppermute(block, axis, route)


def combine(first_vec, second_vec, first_sign, second_sign):
    return tuple((first_sign * first_vec[i] + second_sign * second_vec[i] for i in range(3)))


def acceleration(padded, stiff_shear, stiff_bulk, loading):
    layers = padded.shape[1] - 2
    stripes = padded.shape[2] - 2
    columns = padded.shape[3] - 2

    def shifted_by(offset):
        return padded[
            :,
            1 + offset[0] : 1 + offset[0] + layers,
            1 + offset[1] : 1 + offset[1] + stripes,
            1 + offset[2] : 1 + offset[2] + columns,
        ]

    centre = shifted_by((0, 0, 0))
    laplace = jnp.zeros_like(centre)
    for step_z in (-1, 0, 1):
        for step_y in (-1, 0, 1):
            for step_x in (-1, 0, 1):
                reach = abs(step_z) + abs(step_y) + abs(step_x)
                if reach > 0:
                    weight = (FACE_WEIGHT, EDGE_WEIGHT, CORNER_WEIGHT)[reach - 1]
                    laplace = laplace + weight * (shifted_by((step_z, step_y, step_x)) - centre)
    axis_units = ((0, 0, 1), (0, 1, 0), (1, 0, 0))
    coupled = []
    for component in range(3):
        own_unit = axis_units[component]
        along = (
            shifted_by(own_unit)[component]
            + shifted_by(combine(own_unit, own_unit, -1, 0))[component]
            - 2.0 * centre[component]
        )
        for other in range(3):
            if other != component:
                other_unit = axis_units[other]
                both_up = shifted_by(combine(own_unit, other_unit, 1, 1))[other]
                up_down = shifted_by(combine(own_unit, other_unit, 1, -1))[other]
                down_up = shifted_by(combine(own_unit, other_unit, -1, 1))[other]
                both_down = shifted_by(combine(own_unit, other_unit, -1, -1))[other]
                along = along + 0.25 * (both_up - up_down - down_up + both_down)
        coupled.append(along)
    coupling = jnp.stack(coupled)
    return stiff_shear * laplace + stiff_bulk * coupling + loading


def slab_rim(displaced):
    rimmed = padded_2(displaced, (("slab", 1),), 1)
    return jnp.pad(rimmed, ((0, 0), (0, 0), (1, 1), (1, 1)))


def propagate(status, step_count, time_step, stiff_shear, stiff_bulk, loading, padder):

    def advance(turn_index, current):
        displaced = current[:3]
        velocity = current[3:]
        velocity = velocity + time_step * acceleration(
            padder(displaced), stiff_shear, stiff_bulk, loading
        )
        displaced = displaced + time_step * velocity
        return jnp.concatenate([displaced, velocity], axis=0)

    return lax.fori_loop(0, step_count, advance, status)


def table_pick(table, position):
    return jnp.sum(
        jnp.where(
            jnp.arange(table.shape[0], dtype=jnp.int32) == position, table, jnp.zeros_like(table)
        )
    )


def shards(states, load_shape, zone_ids, zone_shear, zone_lame, amp_table, cycle_index):
    windows = lax.axis_size("win")
    window_index = lax.axis_index("win")
    zone_range = jnp.arange(zone_shear.shape[0], dtype=jnp.int32)
    matches = zone_ids[None] == zone_range[:, None, None, None]
    stiff_shear = jnp.sum(jnp.where(matches, zone_shear[:, None, None, None], 0.0), axis=0)
    lame_first = jnp.sum(jnp.where(matches, zone_lame[:, None, None, None], 0.0), axis=0)
    stiff_bulk = lame_first + stiff_shear
    load_field = load_shape.astype(jnp.float32)
    own_start = states[0]
    loading = table_pick(amp_table, table_pick(cycle_index, window_index)) * load_field
    fine_end = propagate(own_start, FINE, DT_FINE, stiff_shear, stiff_bulk, loading, slab_rim)
    coarse_old = propagate(own_start, COARSE, DT_COARSE, stiff_shear, stiff_bulk, loading, slab_rim)
    correction = fine_end - coarse_old

    def link(turn_index, current):
        advanced = (
            propagate(current, COARSE, DT_COARSE, stiff_shear, stiff_bulk, loading, slab_rim)
            + correction
        )
        received = passed_along(advanced, "win", 1)
        return jnp.where(window_index == 0, own_start, received)

    current = lax.fori_loop(0, windows - 1, link, own_start)
    new_end = (
        propagate(current, COARSE, DT_COARSE, stiff_shear, stiff_bulk, loading, slab_rim)
        + correction
    )
    return new_end[None]


def solution(mesh):
    placed = (
        P("win", None, "slab", None, None),
        P(None, "slab", None, None),
        P("slab", None, None),
        P(),
        P(),
        P(),
        P(),
    )
    return jax.shard_map(
        shards,
        mesh=mesh,
        in_specs=placed,
        out_specs=P("win", None, "slab", None, None),
        check_vma=False,
    )
```

profile of v0, /device:TPU:320, one launch (start us, length us, event | category | flops | bytes accessed | tf_op | source)
XLA Modules:
  0.0 553.5 jit_solution(2632373008691807921)
XLA Ops:
  6.1 74.9 %while.67 = (s32[]{:T(128)}, f32[6,2,64,256]{3,2,1,0:T(8,128)S(1)}, f32[2,64,256]{2,1,0:T(8,128)S(1)}, f32[2,64,256]{2,1,0:T(8,128)S(1)}, f32[3,2,64,256]{3,2,1,0:T(8,128)S(1)}, /*index=5*/s32[]{:T(128)}) while((s32[]{:T(128)}, f32[6,2,64,256]{3,2,1,0:T(8,128)S(1)}, f32[2,64,256]{2,1,0:T(8,128)S(1)}, f32[2,64,256]{2,1,0:T(8,128)S(1)}, ...), condition=%wide.region_5.6_spmd, body=%wide.region_4.5_spmd.sunk | while | flops 13354194 | bytes 24410452 | solution.py:100
  6.2 7.6 %collective-permute-start = (f32[3,1,64,256]{3,2,1,0:T(8,128)S(1)}, f32[3,1,64,256]{3,2,1,0:T(8,128)S(1)}, u32[]{:S(2)}, u32[]{:S(2)}) collective-permute-start(f32[3,1,64,256]{3,2,1,0:T(8,128)S(1)} %get-tuple-element.633), channel_id=1, source_target_pairs={{1,0},{2,1},{3,2},{4,3},{5,4},{6,5},{7,6},{8,7},{9,8},{10,9},{11,1... | collective-permute-start | bytes 589832 | tf_op jit(solution)/shard_map/while/body/eval_jaxpr/ppermute | solution.py:25
  17.9 8.3 %collective-permute-done.1 = f32[3,1,64,256]{3,2,1,0:T(8,128)S(1)} collective-permute-done((f32[3,1,64,256]{3,2,1,0:T(8,128)S(1)}, f32[3,1,64,256]{3,2,1,0:T(8,128)S(1)}, u32[]{:S(2)}, u32[]{:S(2)}) %collective-permute-start.1) | collective-permute-done | bytes 196640 | tf_op jit(solution)/shard_map/while/body/eval_jaxpr/ppermute | solution.py:22
  37.2 6.1 %collective-permute-done.1 = f32[3,1,64,256]{3,2,1,0:T(8,128)S(1)} collective-permute-done((f32[3,1,64,256]{3,2,1,0:T(8,128)S(1)}, f32[3,1,64,256]{3,2,1,0:T(8,128)S(1)}, u32[]{:S(2)}, u32[]{:S(2)}) %collective-permute-start.1) | collective-permute-done | bytes 196640 | tf_op jit(solution)/shard_map/while/body/eval_jaxpr/ppermute | solution.py:22
  48.7 3.9 collective-permute-start.1
  54.3 6.1 %collective-permute-done.1 = f32[3,1,64,256]{3,2,1,0:T(8,128)S(1)} collective-permute-done((f32[3,1,64,256]{3,2,1,0:T(8,128)S(1)}, f32[3,1,64,256]{3,2,1,0:T(8,128)S(1)}, u32[]{:S(2)}, u32[]{:S(2)}) %collective-permute-start.1) | collective-permute-done | bytes 196640 | tf_op jit(solution)/shard_map/while/body/eval_jaxpr/ppermute | solution.py:22
  71.5 6.1 %collective-permute-done.1 = f32[3,1,64,256]{3,2,1,0:T(8,128)S(1)} collective-permute-done((f32[3,1,64,256]{3,2,1,0:T(8,128)S(1)}, f32[3,1,64,256]{3,2,1,0:T(8,128)S(1)}, u32[]{:S(2)}, u32[]{:S(2)}) %collective-permute-start.1) | collective-permute-done | bytes 196640 | tf_op jit(solution)/shard_map/while/body/eval_jaxpr/ppermute | solution.py:22
  81.1 42.0 %while.68 = (s32[]{:T(128)}, f32[6,2,64,256]{3,2,1,0:T(8,128)S(1)}, f32[2,64,256]{2,1,0:T(8,128)S(1)}, f32[2,64,256]{2,1,0:T(8,128)S(1)}, f32[3,2,64,256]{3,2,1,0:T(8,128)S(1)}, /*index=5*/s32[]{:T(128)}) while((s32[]{:T(128)}, f32[6,2,64,256]{3,2,1,0:T(8,128)S(1)}, f32[2,64,256]{2,1,0:T(8,128)S(1)}, f32[2,64,256]{2,1,0:T(8,128)S(1)}, ...), condition=%wide.region_7.8_spmd, body=%wide.region_6.7_spmd.sunk | while | flops 13354194 | bytes 24410452 | solution.py:100
  83.8 3.9 collective-permute-start.3
  89.8 6.1 %collective-permute-done.3 = f32[3,1,64,256]{3,2,1,0:T(8,128)} collective-permute-done((f32[3,1,64,256]{3,2,1,0:T(8,128)}, f32[3,1,64,256]{3,2,1,0:T(8,128)}, u32[]{:S(2)}, u32[]{:S(2)}) %collective-permute-start.3) | collective-permute-done | bytes 196640 | tf_op jit(solution)/shard_map/while/body/eval_jaxpr/ppermute | solution.py:22
  104.8 3.9 collective-permute-start.3
  110.7 6.1 %collective-permute-done.3 = f32[3,1,64,256]{3,2,1,0:T(8,128)} collective-permute-done((f32[3,1,64,256]{3,2,1,0:T(8,128)}, f32[3,1,64,256]{3,2,1,0:T(8,128)}, u32[]{:S(2)}, u32[]{:S(2)}) %collective-permute-start.3) | collective-permute-done | bytes 196640 | tf_op jit(solution)/shard_map/while/body/eval_jaxpr/ppermute | solution.py:22
  124.2 393.9 %while.70 = (s32[]{:T(128)}, f32[6,2,64,256]{3,2,1,0:T(8,128)S(1)}, pred[]{:T(512)}, f32[2,64,256]{2,1,0:T(8,128)S(1)}, f32[2,64,256]{2,1,0:T(8,128)S(1)}, /*ind...) while((s32[]{:T(128)}, f32[6,2,64,256]{3,2,1,0:T(8,128)S(1)}, ...), condition=%wide.region_11.12_spmd, body=%wide.region_8.11_spmd.sunk | while | flops 13747412 | bytes 32274976 | solution.py:134
  124.2 35.3 %while.72 = (s32[]{:T(128)}, f32[6,2,64,256]{3,2,1,0:T(8,128)S(1)}, f32[2,64,256]{2,1,0:T(8,128)S(1)}, f32[2,64,256]{2,1,0:T(8,128)S(1)}, f32[3,2,64,256]{3,2,1,0:T(8,128)S(1)}, /*index=5*/s32[]{:T(128)}) while((s32[]{:T(128)}, f32[6,2,64,256]{3,2,1,0:T(8,128)S(1)}, f32[2,64,256]{2,1,0:T(8,128)S(1)}, f32[2,64,256]{2,1,0:T(8,128)S(1)}, ...), condition=%wide.region_10.10_spmd, body=%wide.region_9.9_spmd.sunk | while | flops 13354194 | bytes 24410452 | solution.py:100
  131.8 6.1 %collective-permute-done.7 = f32[3,1,64,256]{3,2,1,0:T(8,128)S(1)} collective-permute-done((f32[3,1,64,256]{3,2,1,0:T(8,128)S(1)}, f32[3,1,64,256]{3,2,1,0:T(8,128)S(1)}, u32[]{:S(2)}, u32[]{:S(2)}) %collective-permute-start.7) | collective-permute-done | bytes 196640 | tf_op jit(solution)/shard_map/while/body/eval_jaxpr/while/body/eval_jaxpr/ppermute | solution.py:22
  148.9 7.1 %collective-permute-done.7 = f32[3,1,64,256]{3,2,1,0:T(8,128)S(1)} collective-permute-done((f32[3,1,64,256]{3,2,1,0:T(8,128)S(1)}, f32[3,1,64,256]{3,2,1,0:T(8,128)S(1)}, u32[]{:S(2)}, u32[]{:S(2)}) %collective-permute-start.7) | collective-permute-done | bytes 196640 | tf_op jit(solution)/shard_map/while/body/eval_jaxpr/while/body/eval_jaxpr/ppermute | solution.py:22
  163.5 13.8 %collective-permute-done.8 = f32[6,2,64,256]{3,2,1,0:T(8,128)S(1)} collective-permute-done((f32[6,2,64,256]{3,2,1,0:T(8,128)}, f32[6,2,64,256]{3,2,1,0:T(8,128)S(1)}, u32[]{:S(2)}, u32[]{:S(2)}) %collective-permute-start.8) | collective-permute-done | bytes 786464 | tf_op jit(solution)/shard_map/while/body/eval_jaxpr/ppermute | solution.py:33
  177.4 36.5 %while.72 = (s32[]{:T(128)}, f32[6,2,64,256]{3,2,1,0:T(8,128)S(1)}, f32[2,64,256]{2,1,0:T(8,128)S(1)}, f32[2,64,256]{2,1,0:T(8,128)S(1)}, f32[3,2,64,256]{3,2,1,0:T(8,128)S(1)}, /*index=5*/s32[]{:T(128)}) while((s32[]{:T(128)}, f32[6,2,64,256]{3,2,1,0:T(8,128)S(1)}, f32[2,64,256]{2,1,0:T(8,128)S(1)}, f32[2,64,256]{2,1,0:T(8,128)S(1)}, ...), condition=%wide.region_10.10_spmd, body=%wide.region_9.9_spmd.sunk | while | flops 13354194 | bytes 24410452 | solution.py:100
  179.4 3.9 collective-permute-start.7
  185.0 6.1 %collective-permute-done.7 = f32[3,1,64,256]{3,2,1,0:T(8,128)S(1)} collective-permute-done((f32[3,1,64,256]{3,2,1,0:T(8,128)S(1)}, f32[3,1,64,256]{3,2,1,0:T(8,128)S(1)}, u32[]{:S(2)}, u32[]{:S(2)}) %collective-permute-start.7) | collective-permute-done | bytes 196640 | tf_op jit(solution)/shard_map/while/body/eval_jaxpr/while/body/eval_jaxpr/ppermute | solution.py:22
  202.2 8.4 %collective-permute-done.7 = f32[3,1,64,256]{3,2,1,0:T(8,128)S(1)} collective-permute-done((f32[3,1,64,256]{3,2,1,0:T(8,128)S(1)}, f32[3,1,64,256]{3,2,1,0:T(8,128)S(1)}, u32[]{:S(2)}, u32[]{:S(2)}) %collective-permute-start.7) | collective-permute-done | bytes 196640 | tf_op jit(solution)/shard_map/while/body/eval_jaxpr/while/body/eval_jaxpr/ppermute | solution.py:22
  218.0 22.1 %collective-permute-done.8 = f32[6,2,64,256]{3,2,1,0:T(8,128)S(1)} collective-permute-done((f32[6,2,64,256]{3,2,1,0:T(8,128)}, f32[6,2,64,256]{3,2,1,0:T(8,128)S(1)}, u32[]{:S(2)}, u32[]{:S(2)}) %collective-permute-start.8) | collective-permute-done | bytes 786464 | tf_op jit(solution)/shard_map/while/body/eval_jaxpr/ppermute | solution.py:33
  240.3 34.4 %while.72 = (s32[]{:T(128)}, f32[6,2,64,256]{3,2,1,0:T(8,128)S(1)}, f32[2,64,256]{2,1,0:T(8,128)S(1)}, f32[2,64,256]{2,1,0:T(8,128)S(1)}, f32[3,2,64,256]{3,2,1,0:T(8,128)S(1)}, /*index=5*/s32[]{:T(128)}) while((s32[]{:T(128)}, f32[6,2,64,256]{3,2,1,0:T(8,128)S(1)}, f32[2,64,256]{2,1,0:T(8,128)S(1)}, f32[2,64,256]{2,1,0:T(8,128)S(1)}, ...), condition=%wide.region_10.10_spmd, body=%wide.region_9.9_spmd.sunk | while | flops 13354194 | bytes 24410452 | solution.py:100
  247.9 6.1 %collective-permute-done.7 = f32[3,1,64,256]{3,2,1,0:T(8,128)S(1)} collective-permute-done((f32[3,1,64,256]{3,2,1,0:T(8,128)S(1)}, f32[3,1,64,256]{3,2,1,0:T(8,128)S(1)}, u32[]{:S(2)}, u32[]{:S(2)}) %collective-permute-start.7) | collective-permute-done | bytes 196640 | tf_op jit(solution)/shard_map/while/body/eval_jaxpr/while/body/eval_jaxpr/ppermute | solution.py:22
  259.4 3.9 collective-permute-start.7
  265.0 6.2 %collective-permute-done.7 = f32[3,1,64,256]{3,2,1,0:T(8,128)S(1)} collective-permute-done((f32[3,1,64,256]{3,2,1,0:T(8,128)S(1)}, f32[3,1,64,256]{3,2,1,0:T(8,128)S(1)}, u32[]{:S(2)}, u32[]{:S(2)}) %collective-permute-start.7) | collective-permute-done | bytes 196640 | tf_op jit(solution)/shard_map/while/body/eval_jaxpr/while/body/eval_jaxpr/ppermute | solution.py:22
  278.7 13.7 %collective-permute-done.8 = f32[6,2,64,256]{3,2,1,0:T(8,128)S(1)} collective-permute-done((f32[6,2,64,256]{3,2,1,0:T(8,128)}, f32[6,2,64,256]{3,2,1,0:T(8,128)S(1)}, u32[]{:S(2)}, u32[]{:S(2)}) %collective-permute-start.8) | collective-permute-done | bytes 786464 | tf_op jit(solution)/shard_map/while/body/eval_jaxpr/ppermute | solution.py:33
  292.5 36.2 %while.72 = (s32[]{:T(128)}, f32[6,2,64,256]{3,2,1,0:T(8,128)S(1)}, f32[2,64,256]{2,1,0:T(8,128)S(1)}, f32[2,64,256]{2,1,0:T(8,128)S(1)}, f32[3,2,64,256]{3,2,1,0:T(8,128)S(1)}, /*index=5*/s32[]{:T(128)}) while((s32[]{:T(128)}, f32[6,2,64,256]{3,2,1,0:T(8,128)S(1)}, f32[2,64,256]{2,1,0:T(8,128)S(1)}, f32[2,64,256]{2,1,0:T(8,128)S(1)}, ...), condition=%wide.region_10.10_spmd, body=%wide.region_9.9_spmd.sunk | while | flops 13354194 | bytes 24410452 | solution.py:100
  294.5 7.3 %collective-permute-start.7 = (f32[3,1,64,256]{3,2,1,0:T(8,128)S(1)}, f32[3,1,64,256]{3,2,1,0:T(8,128)S(1)}, u32[]{:S(2)}, u32[]{:S(2)}) collective-permute-start(f32[3,1,64,256]{3,2,1,0:T(8,128)S(1)} %get-tuple-element.671), channel_id=1, source_target_pairs={{0,1},{1,2},{2,3},{3,4},{4,5},{5,6},{6,7},{7,8},{8,9},{9,10},{10,1... | collective-permute-start | bytes 589832 | tf_op jit(solution)/shard_map/while/body/eval_jaxpr/while/body/eval_jaxpr/ppermute | solution.py:22
  317.3 8.1 %collective-permute-done.7 = f32[3,1,64,256]{3,2,1,0:T(8,128)S(1)} collective-permute-done((f32[3,1,64,256]{3,2,1,0:T(8,128)S(1)}, f32[3,1,64,256]{3,2,1,0:T(8,128)S(1)}, u32[]{:S(2)}, u32[]{:S(2)}) %collective-permute-start.7) | collective-permute-done | bytes 196640 | tf_op jit(solution)/shard_map/while/body/eval_jaxpr/while/body/eval_jaxpr/ppermute | solution.py:22
  332.8 22.0 %collective-permute-done.8 = f32[6,2,64,256]{3,2,1,0:T(8,128)S(1)} collective-permute-done((f32[6,2,64,256]{3,2,1,0:T(8,128)}, f32[6,2,64,256]{3,2,1,0:T(8,128)S(1)}, u32[]{:S(2)}, u32[]{:S(2)}) %collective-permute-start.8) | collective-permute-done | bytes 786464 | tf_op jit(solution)/shard_map/while/body/eval_jaxpr/ppermute | solution.py:33
  354.9 36.3 %while.72 = (s32[]{:T(128)}, f32[6,2,64,256]{3,2,1,0:T(8,128)S(1)}, f32[2,64,256]{2,1,0:T(8,128)S(1)}, f32[2,64,256]{2,1,0:T(8,128)S(1)}, f32[3,2,64,256]{3,2,1,0:T(8,128)S(1)}, /*index=5*/s32[]{:T(128)}) while((s32[]{:T(128)}, f32[6,2,64,256]{3,2,1,0:T(8,128)S(1)}, f32[2,64,256]{2,1,0:T(8,128)S(1)}, f32[2,64,256]{2,1,0:T(8,128)S(1)}, ...), condition=%wide.region_10.10_spmd, body=%wide.region_9.9_spmd.sunk | while | flops 13354194 | bytes 24410452 | solution.py:100
  356.9 3.9 collective-permute-start.7
  363.4 6.1 %collective-permute-done.7 = f32[3,1,64,256]{3,2,1,0:T(8,128)S(1)} collective-permute-done((f32[3,1,64,256]{3,2,1,0:T(8,128)S(1)}, f32[3,1,64,256]{3,2,1,0:T(8,128)S(1)}, u32[]{:S(2)}, u32[]{:S(2)}) %collective-permute-start.7) | collective-permute-done | bytes 196640 | tf_op jit(solution)/shard_map/while/body/eval_jaxpr/while/body/eval_jaxpr/ppermute | solution.py:22
  375.0 3.9 collective-permute-start.7
  380.6 7.2 %collective-permute-done.7 = f32[3,1,64,256]{3,2,1,0:T(8,128)S(1)} collective-permute-done((f32[3,1,64,256]{3,2,1,0:T(8,128)S(1)}, f32[3,1,64,256]{3,2,1,0:T(8,128)S(1)}, u32[]{:S(2)}, u32[]{:S(2)}) %collective-permute-start.7) | collective-permute-done | bytes 196640 | tf_op jit(solution)/shard_map/while/body/eval_jaxpr/while/body/eval_jaxpr/ppermute | solution.py:22
  395.2 14.1 %collective-permute-done.8 = f32[6,2,64,256]{3,2,1,0:T(8,128)S(1)} collective-permute-done((f32[6,2,64,256]{3,2,1,0:T(8,128)}, f32[6,2,64,256]{3,2,1,0:T(8,128)S(1)}, u32[]{:S(2)}, u32[]{:S(2)}) %collective-permute-start.8) | collective-permute-done | bytes 786464 | tf_op jit(solution)/shard_map/while/body/eval_jaxpr/ppermute | solution.py:33
  409.4 36.4 %while.72 = (s32[]{:T(128)}, f32[6,2,64,256]{3,2,1,0:T(8,128)S(1)}, f32[2,64,256]{2,1,0:T(8,128)S(1)}, f32[2,64,256]{2,1,0:T(8,128)S(1)}, f32[3,2,64,256]{3,2,1,0:T(8,128)S(1)}, /*index=5*/s32[]{:T(128)}) while((s32[]{:T(128)}, f32[6,2,64,256]{3,2,1,0:T(8,128)S(1)}, f32[2,64,256]{2,1,0:T(8,128)S(1)}, f32[2,64,256]{2,1,0:T(8,128)S(1)}, ...), condition=%wide.region_10.10_spmd, body=%wide.region_9.9_spmd.sunk | while | flops 13354194 | bytes 24410452 | solution.py:100
  417.0 6.1 %collective-permute-done.7 = f32[3,1,64,256]{3,2,1,0:T(8,128)S(1)} collective-permute-done((f32[3,1,64,256]{3,2,1,0:T(8,128)S(1)}, f32[3,1,64,256]{3,2,1,0:T(8,128)S(1)}, u32[]{:S(2)}, u32[]{:S(2)}) %collective-permute-start.7) | collective-permute-done | bytes 196640 | tf_op jit(solution)/shard_map/while/body/eval_jaxpr/while/body/eval_jaxpr/ppermute | solution.py:22
  434.2 8.3 %collective-permute-done.7 = f32[3,1,64,256]{3,2,1,0:T(8,128)S(1)} collective-permute-done((f32[3,1,64,256]{3,2,1,0:T(8,128)S(1)}, f32[3,1,64,256]{3,2,1,0:T(8,128)S(1)}, u32[]{:S(2)}, u32[]{:S(2)}) %collective-permute-start.7) | collective-permute-done | bytes 196640 | tf_op jit(solution)/shard_map/while/body/eval_jaxpr/while/body/eval_jaxpr/ppermute | solution.py:22
  449.9 13.7 %collective-permute-done.8 = f32[6,2,64,256]{3,2,1,0:T(8,128)S(1)} collective-permute-done((f32[6,2,64,256]{3,2,1,0:T(8,128)}, f32[6,2,64,256]{3,2,1,0:T(8,128)S(1)}, u32[]{:S(2)}, u32[]{:S(2)}) %collective-permute-start.8) | collective-permute-done | bytes 786464 | tf_op jit(solution)/shard_map/while/body/eval_jaxpr/ppermute | solution.py:33
  463.7 36.4 %while.72 = (s32[]{:T(128)}, f32[6,2,64,256]{3,2,1,0:T(8,128)S(1)}, f32[2,64,256]{2,1,0:T(8,128)S(1)}, f32[2,64,256]{2,1,0:T(8,128)S(1)}, f32[3,2,64,256]{3,2,1,0:T(8,128)S(1)}, /*index=5*/s32[]{:T(128)}) while((s32[]{:T(128)}, f32[6,2,64,256]{3,2,1,0:T(8,128)S(1)}, f32[2,64,256]{2,1,0:T(8,128)S(1)}, f32[2,64,256]{2,1,0:T(8,128)S(1)}, ...), condition=%wide.region_10.10_spmd, body=%wide.region_9.9_spmd.sunk | while | flops 13354194 | bytes 24410452 | solution.py:100
  471.4 6.1 %collective-permute-done.7 = f32[3,1,64,256]{3,2,1,0:T(8,128)S(1)} collective-permute-done((f32[3,1,64,256]{3,2,1,0:T(8,128)S(1)}, f32[3,1,64,256]{3,2,1,0:T(8,128)S(1)}, u32[]{:S(2)}, u32[]{:S(2)}) %collective-permute-start.7) | collective-permute-done | bytes 196640 | tf_op jit(solution)/shard_map/while/body/eval_jaxpr/while/body/eval_jaxpr/ppermute | solution.py:22
  488.5 8.3 %collective-permute-done.7 = f32[3,1,64,256]{3,2,1,0:T(8,128)S(1)} collective-permute-done((f32[3,1,64,256]{3,2,1,0:T(8,128)S(1)}, f32[3,1,64,256]{3,2,1,0:T(8,128)S(1)}, u32[]{:S(2)}, u32[]{:S(2)}) %collective-permute-start.7) | collective-permute-done | bytes 196640 | tf_op jit(solution)/shard_map/while/body/eval_jaxpr/while/body/eval_jaxpr/ppermute | solution.py:22
  504.2 13.7 %collective-permute-done.8 = f32[6,2,64,256]{3,2,1,0:T(8,128)S(1)} collective-permute-done((f32[6,2,64,256]{3,2,1,0:T(8,128)}, f32[6,2,64,256]{3,2,1,0:T(8,128)S(1)}, u32[]{:S(2)}, u32[]{:S(2)}) %collective-permute-start.8) | collective-permute-done | bytes 786464 | tf_op jit(solution)/shard_map/while/body/eval_jaxpr/ppermute | solution.py:33
  518.1 34.4 %while.71 = (s32[]{:T(128)}, f32[6,2,64,256]{3,2,1,0:T(8,128)S(1)}, f32[2,64,256]{2,1,0:T(8,128)S(1)}, f32[2,64,256]{2,1,0:T(8,128)S(1)}, f32[3,2,64,256]{3,2,1,0:T(8,128)S(1)}, /*index=5*/s32[]{:T(128)}) while((s32[]{:T(128)}, f32[6,2,64,256]{3,2,1,0:T(8,128)S(1)}, f32[2,64,256]{2,1,0:T(8,128)S(1)}, f32[2,64,256]{2,1,0:T(8,128)S(1)}, ...), condition=%wide.region_13.14_spmd, body=%wide.region_12.13_spmd.sunk | while | flops 13354194 | bytes 24410452 | solution.py:100
  525.8 6.1 %collective-permute-done.5 = f32[3,1,64,256]{3,2,1,0:T(8,128)S(1)} collective-permute-done((f32[3,1,64,256]{3,2,1,0:T(8,128)S(1)}, f32[3,1,64,256]{3,2,1,0:T(8,128)S(1)}, u32[]{:S(2)}, u32[]{:S(2)}) %collective-permute-start.5) | collective-permute-done | bytes 196640 | tf_op jit(solution)/shard_map/while/body/eval_jaxpr/ppermute | solution.py:22
  543.0 6.1 %collective-permute-done.5 = f32[3,1,64,256]{3,2,1,0:T(8,128)S(1)} collective-permute-done((f32[3,1,64,256]{3,2,1,0:T(8,128)S(1)}, f32[3,1,64,256]{3,2,1,0:T(8,128)S(1)}, u32[]{:S(2)}, u32[]{:S(2)}) %collective-permute-start.5) | collective-permute-done | bytes 196640 | tf_op jit(solution)/shard_map/while/body/eval_jaxpr/ppermute | solution.py:22
  (269 shorter events, 254.1 us)
Async XLA Ops:
  6.2 11.7 %collective-permute-start = (f32[3,1,64,256]{3,2,1,0:T(8,128)S(1)}, f32[3,1,64,256]{3,2,1,0:T(8,128)S(1)}, u32[]{:S(2)}, u32[]{:S(2)}) collective-permute-start(f32[3,1,64,256]{3,2,1,0:T(8,128)S(1)} %get-tuple-element.633), channel_id=1, source_target_pairs={{1,0},{2,1},{3,2},{4,3},{5,4},{6,5},{7,6},{8,7},{9,8},{10,9},{11,1... | collective-permute-start | bytes 589832 | tf_op jit(solution)/shard_map/while/body/eval_jaxpr/ppermute | solution.py:25
  13.7 12.5 %collective-permute-start.1 = (f32[3,1,64,256]{3,2,1,0:T(8,128)S(1)}, f32[3,1,64,256]{3,2,1,0:T(8,128)S(1)}, u32[]{:S(2)}, u32[]{:S(2)}) collective-permute-start(f32[3,1,64,256]{3,2,1,0:T(8,128)S(1)} %get-tuple-element.634), channel_id=1, source_target_pairs={{0,1},{1,2},{2,3},{3,4},{4,5},{5,6},{6,7},{7,8},{8,9},{9,10},{10,1... | collective-permute-start | bytes 589832 | tf_op jit(solution)/shard_map/while/body/eval_jaxpr/ppermute | solution.py:22
  29.6 7.6 %collective-permute-start = (f32[3,1,64,256]{3,2,1,0:T(8,128)S(1)}, f32[3,1,64,256]{3,2,1,0:T(8,128)S(1)}, u32[]{:S(2)}, u32[]{:S(2)}) collective-permute-start(f32[3,1,64,256]{3,2,1,0:T(8,128)S(1)} %get-tuple-element.633), channel_id=1, source_target_pairs={{1,0},{2,1},{3,2},{4,3},{5,4},{6,5},{7,6},{8,7},{9,8},{10,9},{11,1... | collective-permute-start | bytes 589832 | tf_op jit(solution)/shard_map/while/body/eval_jaxpr/ppermute | solution.py:25
  31.6 11.8 %collective-permute-start.1 = (f32[3,1,64,256]{3,2,1,0:T(8,128)S(1)}, f32[3,1,64,256]{3,2,1,0:T(8,128)S(1)}, u32[]{:S(2)}, u32[]{:S(2)}) collective-permute-start(f32[3,1,64,256]{3,2,1,0:T(8,128)S(1)} %get-tuple-element.634), channel_id=1, source_target_pairs={{0,1},{1,2},{2,3},{3,4},{4,5},{5,6},{6,7},{7,8},{8,9},{9,10},{10,1... | collective-permute-start | bytes 589832 | tf_op jit(solution)/shard_map/while/body/eval_jaxpr/ppermute | solution.py:22
  46.8 7.6 %collective-permute-start = (f32[3,1,64,256]{3,2,1,0:T(8,128)S(1)}, f32[3,1,64,256]{3,2,1,0:T(8,128)S(1)}, u32[]{:S(2)}, u32[]{:S(2)}) collective-permute-start(f32[3,1,64,256]{3,2,1,0:T(8,128)S(1)} %get-tuple-element.633), channel_id=1, source_target_pairs={{1,0},{2,1},{3,2},{4,3},{5,4},{6,5},{7,6},{8,7},{9,8},{10,9},{11,1... | collective-permute-start | bytes 589832 | tf_op jit(solution)/shard_map/while/body/eval_jaxpr/ppermute | solution.py:25
  48.7 11.8 %collective-permute-start.1 = (f32[3,1,64,256]{3,2,1,0:T(8,128)S(1)}, f32[3,1,64,256]{3,2,1,0:T(8,128)S(1)}, u32[]{:S(2)}, u32[]{:S(2)}) collective-permute-start(f32[3,1,64,256]{3,2,1,0:T(8,128)S(1)} %get-tuple-element.634), channel_id=1, source_target_pairs={{0,1},{1,2},{2,3},{3,4},{4,5},{5,6},{6,7},{7,8},{8,9},{9,10},{10,1... | collective-permute-start | bytes 589832 | tf_op jit(solution)/shard_map/while/body/eval_jaxpr/ppermute | solution.py:22
  63.9 7.6 %collective-permute-start = (f32[3,1,64,256]{3,2,1,0:T(8,128)S(1)}, f32[3,1,64,256]{3,2,1,0:T(8,128)S(1)}, u32[]{:S(2)}, u32[]{:S(2)}) collective-permute-start(f32[3,1,64,256]{3,2,1,0:T(8,128)S(1)} %get-tuple-element.633), channel_id=1, source_target_pairs={{1,0},{2,1},{3,2},{4,3},{5,4},{6,5},{7,6},{8,7},{9,8},{10,9},{11,1... | collective-permute-start | bytes 589832 | tf_op jit(solution)/shard_map/while/body/eval_jaxpr/ppermute | solution.py:25
  65.8 11.8 %collective-permute-start.1 = (f32[3,1,64,256]{3,2,1,0:T(8,128)S(1)}, f32[3,1,64,256]{3,2,1,0:T(8,128)S(1)}, u32[]{:S(2)}, u32[]{:S(2)}) collective-permute-start(f32[3,1,64,256]{3,2,1,0:T(8,128)S(1)} %get-tuple-element.634), channel_id=1, source_target_pairs={{0,1},{1,2},{2,3},{3,4},{4,5},{5,6},{6,7},{7,8},{8,9},{9,10},{10,1... | collective-permute-start | bytes 589832 | tf_op jit(solution)/shard_map/while/body/eval_jaxpr/ppermute | solution.py:22
  81.9 7.9 %collective-permute-start.2 = (f32[3,1,64,256]{3,2,1,0:T(8,128)}, f32[3,1,64,256]{3,2,1,0:T(8,128)}, u32[]{:S(2)}, u32[]{:S(2)}) collective-permute-start(f32[3,1,64,256]{3,2,1,0:T(8,128)} %get-tuple-element.642), channel_id=1, source_target_pairs={{1,0},{2,1},{3,2},{4,3},{5,4},{6,5},{7,6},{8,7},{9,8},{10,9},{11,1... | collective-permute-start | bytes 589832 | tf_op jit(solution)/shard_map/while/body/eval_jaxpr/ppermute | solution.py:25
  83.8 12.1 %collective-permute-start.3 = (f32[3,1,64,256]{3,2,1,0:T(8,128)}, f32[3,1,64,256]{3,2,1,0:T(8,128)}, u32[]{:S(2)}, u32[]{:S(2)}) collective-permute-start(f32[3,1,64,256]{3,2,1,0:T(8,128)} %get-tuple-element.643), channel_id=1, source_target_pairs={{0,1},{1,2},{2,3},{3,4},{4,5},{5,6},{6,7},{7,8},{8,9},{9,10},{10,1... | collective-permute-start | bytes 589832 | tf_op jit(solution)/shard_map/while/body/eval_jaxpr/ppermute | solution.py:22
  102.9 7.9 %collective-permute-start.2 = (f32[3,1,64,256]{3,2,1,0:T(8,128)}, f32[3,1,64,256]{3,2,1,0:T(8,128)}, u32[]{:S(2)}, u32[]{:S(2)}) collective-permute-start(f32[3,1,64,256]{3,2,1,0:T(8,128)} %get-tuple-element.642), channel_id=1, source_target_pairs={{1,0},{2,1},{3,2},{4,3},{5,4},{6,5},{7,6},{8,7},{9,8},{10,9},{11,1... | collective-permute-start | bytes 589832 | tf_op jit(solution)/shard_map/while/body/eval_jaxpr/ppermute | solution.py:25
  104.8 12.1 %collective-permute-start.3 = (f32[3,1,64,256]{3,2,1,0:T(8,128)}, f32[3,1,64,256]{3,2,1,0:T(8,128)}, u32[]{:S(2)}, u32[]{:S(2)}) collective-permute-start(f32[3,1,64,256]{3,2,1,0:T(8,128)} %get-tuple-element.643), channel_id=1, source_target_pairs={{0,1},{1,2},{2,3},{3,4},{4,5},{5,6},{6,7},{7,8},{8,9},{9,10},{10,1... | collective-permute-start | bytes 589832 | tf_op jit(solution)/shard_map/while/body/eval_jaxpr/ppermute | solution.py:22
  124.2 7.6 %collective-permute-start.6 = (f32[3,1,64,256]{3,2,1,0:T(8,128)S(1)}, f32[3,1,64,256]{3,2,1,0:T(8,128)S(1)}, u32[]{:S(2)}, u32[]{:S(2)}) collective-permute-start(f32[3,1,64,256]{3,2,1,0:T(8,128)S(1)} %get-tuple-element.670), channel_id=1, source_target_pairs={{1,0},{2,1},{3,2},{4,3},{5,4},{6,5},{7,6},{8,7},{9,8},{10,9},{11,1... | collective-permute-start | bytes 589832 | tf_op jit(solution)/shard_map/while/body/eval_jaxpr/while/body/eval_jaxpr/ppermute | solution.py:25
  126.1 11.8 %collective-permute-start.7 = (f32[3,1,64,256]{3,2,1,0:T(8,128)S(1)}, f32[3,1,64,256]{3,2,1,0:T(8,128)S(1)}, u32[]{:S(2)}, u32[]{:S(2)}) collective-permute-start(f32[3,1,64,256]{3,2,1,0:T(8,128)S(1)} %get-tuple-element.671), channel_id=1, source_target_pairs={{0,1},{1,2},{2,3},{3,4},{4,5},{5,6},{6,7},{7,8},{8,9},{9,10},{10,1... | collective-permute-start | bytes 589832 | tf_op jit(solution)/shard_map/while/body/eval_jaxpr/while/body/eval_jaxpr/ppermute | solution.py:22
  141.4 7.6 %collective-permute-start.6 = (f32[3,1,64,256]{3,2,1,0:T(8,128)S(1)}, f32[3,1,64,256]{3,2,1,0:T(8,128)S(1)}, u32[]{:S(2)}, u32[]{:S(2)}) collective-permute-start(f32[3,1,64,256]{3,2,1,0:T(8,128)S(1)} %get-tuple-element.670), channel_id=1, source_target_pairs={{1,0},{2,1},{3,2},{4,3},{5,4},{6,5},{7,6},{8,7},{9,8},{10,9},{11,1... | collective-permute-start | bytes 589832 | tf_op jit(solution)/shard_map/while/body/eval_jaxpr/while/body/eval_jaxpr/ppermute | solution.py:25
  143.3 12.8 %collective-permute-start.7 = (f32[3,1,64,256]{3,2,1,0:T(8,128)S(1)}, f32[3,1,64,256]{3,2,1,0:T(8,128)S(1)}, u32[]{:S(2)}, u32[]{:S(2)}) collective-permute-start(f32[3,1,64,256]{3,2,1,0:T(8,128)S(1)} %get-tuple-element.671), channel_id=1, source_target_pairs={{0,1},{1,2},{2,3},{3,4},{4,5},{5,6},{6,7},{7,8},{8,9},{9,10},{10,1... | collective-permute-start | bytes 589832 | tf_op jit(solution)/shard_map/while/body/eval_jaxpr/while/body/eval_jaxpr/ppermute | solution.py:22
  161.6 15.7 %collective-permute-start.8 = (f32[6,2,64,256]{3,2,1,0:T(8,128)}, f32[6,2,64,256]{3,2,1,0:T(8,128)S(1)}, u32[]{:S(2)}, u32[]{:S(2)}) collective-permute-start(f32[6,2,64,256]{3,2,1,0:T(8,128)} %add.3322), channel_id=1, source_target_pairs={{0,64},{64,128},{128,192},{192,256},{256,320},{320,384},{384,448},... | collective-permute-start | bytes 2359304 | tf_op jit(solution)/shard_map/while/body/eval_jaxpr/ppermute | solution.py:33
  177.5 7.6 %collective-permute-start.6 = (f32[3,1,64,256]{3,2,1,0:T(8,128)S(1)}, f32[3,1,64,256]{3,2,1,0:T(8,128)S(1)}, u32[]{:S(2)}, u32[]{:S(2)}) collective-permute-start(f32[3,1,64,256]{3,2,1,0:T(8,128)S(1)} %get-tuple-element.670), channel_id=1, source_target_pairs={{1,0},{2,1},{3,2},{4,3},{5,4},{6,5},{7,6},{8,7},{9,8},{10,9},{11,1... | collective-permute-start | bytes 589832 | tf_op jit(solution)/shard_map/while/body/eval_jaxpr/while/body/eval_jaxpr/ppermute | solution.py:25
  179.4 11.8 %collective-permute-start.7 = (f32[3,1,64,256]{3,2,1,0:T(8,128)S(1)}, f32[3,1,64,256]{3,2,1,0:T(8,128)S(1)}, u32[]{:S(2)}, u32[]{:S(2)}) collective-permute-start(f32[3,1,64,256]{3,2,1,0:T(8,128)S(1)} %get-tuple-element.671), channel_id=1, source_target_pairs={{0,1},{1,2},{2,3},{3,4},{4,5},{5,6},{6,7},{7,8},{8,9},{9,10},{10,1... | collective-permute-start | bytes 589832 | tf_op jit(solution)/shard_map/while/body/eval_jaxpr/while/body/eval_jaxpr/ppermute | solution.py:22
  194.6 7.6 %collective-permute-start.6 = (f32[3,1,64,256]{3,2,1,0:T(8,128)S(1)}, f32[3,1,64,256]{3,2,1,0:T(8,128)S(1)}, u32[]{:S(2)}, u32[]{:S(2)}) collective-permute-start(f32[3,1,64,256]{3,2,1,0:T(8,128)S(1)} %get-tuple-element.670), channel_id=1, source_target_pairs={{1,0},{2,1},{3,2},{4,3},{5,4},{6,5},{7,6},{8,7},{9,8},{10,9},{11,1... | collective-permute-start | bytes 589832 | tf_op jit(solution)/shard_map/while/body/eval_jaxpr/while/body/eval_jaxpr/ppermute | solution.py:25
  196.5 14.0 %collective-permute-start.7 = (f32[3,1,64,256]{3,2,1,0:T(8,128)S(1)}, f32[3,1,64,256]{3,2,1,0:T(8,128)S(1)}, u32[]{:S(2)}, u32[]{:S(2)}) collective-permute-start(f32[3,1,64,256]{3,2,1,0:T(8,128)S(1)} %get-tuple-element.671), channel_id=1, source_target_pairs={{0,1},{1,2},{2,3},{3,4},{4,5},{5,6},{6,7},{7,8},{8,9},{9,10},{10,1... | collective-permute-start | bytes 589832 | tf_op jit(solution)/shard_map/while/body/eval_jaxpr/while/body/eval_jaxpr/ppermute | solution.py:22
  216.1 24.0 %collective-permute-start.8 = (f32[6,2,64,256]{3,2,1,0:T(8,128)}, f32[6,2,64,256]{3,2,1,0:T(8,128)S(1)}, u32[]{:S(2)}, u32[]{:S(2)}) collective-permute-start(f32[6,2,64,256]{3,2,1,0:T(8,128)} %add.3322), channel_id=1, source_target_pairs={{0,64},{64,128},{128,192},{192,256},{256,320},{320,384},{384,448},... | collective-permute-start | bytes 2359304 | tf_op jit(solution)/shard_map/while/body/eval_jaxpr/ppermute | solution.py:33
  240.3 7.6 %collective-permute-start.6 = (f32[3,1,64,256]{3,2,1,0:T(8,128)S(1)}, f32[3,1,64,256]{3,2,1,0:T(8,128)S(1)}, u32[]{:S(2)}, u32[]{:S(2)}) collective-permute-start(f32[3,1,64,256]{3,2,1,0:T(8,128)S(1)} %get-tuple-element.670), channel_id=1, source_target_pairs={{1,0},{2,1},{3,2},{4,3},{5,4},{6,5},{7,6},{8,7},{9,8},{10,9},{11,1... | collective-permute-start | bytes 589832 | tf_op jit(solution)/shard_map/while/body/eval_jaxpr/while/body/eval_jaxpr/ppermute | solution.py:25
  242.2 11.8 %collective-permute-start.7 = (f32[3,1,64,256]{3,2,1,0:T(8,128)S(1)}, f32[3,1,64,256]{3,2,1,0:T(8,128)S(1)}, u32[]{:S(2)}, u32[]{:S(2)}) collective-permute-start(f32[3,1,64,256]{3,2,1,0:T(8,128)S(1)} %get-tuple-element.671), channel_id=1, source_target_pairs={{0,1},{1,2},{2,3},{3,4},{4,5},{5,6},{6,7},{7,8},{8,9},{9,10},{10,1... | collective-permute-start | bytes 589832 | tf_op jit(solution)/shard_map/while/body/eval_jaxpr/while/body/eval_jaxpr/ppermute | solution.py:22
  257.5 7.6 %collective-permute-start.6 = (f32[3,1,64,256]{3,2,1,0:T(8,128)S(1)}, f32[3,1,64,256]{3,2,1,0:T(8,128)S(1)}, u32[]{:S(2)}, u32[]{:S(2)}) collective-permute-start(f32[3,1,64,256]{3,2,1,0:T(8,128)S(1)} %get-tuple-element.670), channel_id=1, source_target_pairs={{1,0},{2,1},{3,2},{4,3},{5,4},{6,5},{7,6},{8,7},{9,8},{10,9},{11,1... | collective-permute-start | bytes 589832 | tf_op jit(solution)/shard_map/while/body/eval_jaxpr/while/body/eval_jaxpr/ppermute | solution.py:25
  259.4 11.9 %collective-permute-start.7 = (f32[3,1,64,256]{3,2,1,0:T(8,128)S(1)}, f32[3,1,64,256]{3,2,1,0:T(8,128)S(1)}, u32[]{:S(2)}, u32[]{:S(2)}) collective-permute-start(f32[3,1,64,256]{3,2,1,0:T(8,128)S(1)} %get-tuple-element.671), channel_id=1, source_target_pairs={{0,1},{1,2},{2,3},{3,4},{4,5},{5,6},{6,7},{7,8},{8,9},{9,10},{10,1... | collective-permute-start | bytes 589832 | tf_op jit(solution)/shard_map/while/body/eval_jaxpr/while/body/eval_jaxpr/ppermute | solution.py:22
  276.8 15.6 %collective-permute-start.8 = (f32[6,2,64,256]{3,2,1,0:T(8,128)}, f32[6,2,64,256]{3,2,1,0:T(8,128)S(1)}, u32[]{:S(2)}, u32[]{:S(2)}) collective-permute-start(f32[6,2,64,256]{3,2,1,0:T(8,128)} %add.3322), channel_id=1, source_target_pairs={{0,64},{64,128},{128,192},{192,256},{256,320},{320,384},{384,448},... | collective-permute-start | bytes 2359304 | tf_op jit(solution)/shard_map/while/body/eval_jaxpr/ppermute | solution.py:33
  292.6 10.9 %collective-permute-start.6 = (f32[3,1,64,256]{3,2,1,0:T(8,128)S(1)}, f32[3,1,64,256]{3,2,1,0:T(8,128)S(1)}, u32[]{:S(2)}, u32[]{:S(2)}) collective-permute-start(f32[3,1,64,256]{3,2,1,0:T(8,128)S(1)} %get-tuple-element.670), channel_id=1, source_target_pairs={{1,0},{2,1},{3,2},{4,3},{5,4},{6,5},{7,6},{8,7},{9,8},{10,9},{11,1... | collective-permute-start | bytes 589832 | tf_op jit(solution)/shard_map/while/body/eval_jaxpr/while/body/eval_jaxpr/ppermute | solution.py:25
  294.5 11.8 %collective-permute-start.7 = (f32[3,1,64,256]{3,2,1,0:T(8,128)S(1)}, f32[3,1,64,256]{3,2,1,0:T(8,128)S(1)}, u32[]{:S(2)}, u32[]{:S(2)}) collective-permute-start(f32[3,1,64,256]{3,2,1,0:T(8,128)S(1)} %get-tuple-element.671), channel_id=1, source_target_pairs={{0,1},{1,2},{2,3},{3,4},{4,5},{5,6},{6,7},{7,8},{8,9},{9,10},{10,1... | collective-permute-start | bytes 589832 | tf_op jit(solution)/shard_map/while/body/eval_jaxpr/while/body/eval_jaxpr/ppermute | solution.py:22
  309.7 7.6 %collective-permute-start.6 = (f32[3,1,64,256]{3,2,1,0:T(8,128)S(1)}, f32[3,1,64,256]{3,2,1,0:T(8,128)S(1)}, u32[]{:S(2)}, u32[]{:S(2)}) collective-permute-start(f32[3,1,64,256]{3,2,1,0:T(8,128)S(1)} %get-tuple-element.670), channel_id=1, source_target_pairs={{1,0},{2,1},{3,2},{4,3},{5,4},{6,5},{7,6},{8,7},{9,8},{10,9},{11,1... | collective-permute-start | bytes 589832 | tf_op jit(solution)/shard_map/while/body/eval_jaxpr/while/body/eval_jaxpr/ppermute | solution.py:25
  311.6 13.7 %collective-permute-start.7 = (f32[3,1,64,256]{3,2,1,0:T(8,128)S(1)}, f32[3,1,64,256]{3,2,1,0:T(8,128)S(1)}, u32[]{:S(2)}, u32[]{:S(2)}) collective-permute-start(f32[3,1,64,256]{3,2,1,0:T(8,128)S(1)} %get-tuple-element.671), channel_id=1, source_target_pairs={{0,1},{1,2},{2,3},{3,4},{4,5},{5,6},{6,7},{7,8},{8,9},{9,10},{10,1... | collective-permute-start | bytes 589832 | tf_op jit(solution)/shard_map/while/body/eval_jaxpr/while/body/eval_jaxpr/ppermute | solution.py:22
  330.9 23.9 %collective-permute-start.8 = (f32[6,2,64,256]{3,2,1,0:T(8,128)}, f32[6,2,64,256]{3,2,1,0:T(8,128)S(1)}, u32[]{:S(2)}, u32[]{:S(2)}) collective-permute-start(f32[6,2,64,256]{3,2,1,0:T(8,128)} %add.3322), channel_id=1, source_target_pairs={{0,64},{64,128},{128,192},{192,256},{256,320},{320,384},{384,448},... | collective-permute-start | bytes 2359304 | tf_op jit(solution)/shard_map/while/body/eval_jaxpr/ppermute | solution.py:33
  355.0 8.5 %collective-permute-start.6 = (f32[3,1,64,256]{3,2,1,0:T(8,128)S(1)}, f32[3,1,64,256]{3,2,1,0:T(8,128)S(1)}, u32[]{:S(2)}, u32[]{:S(2)}) collective-permute-start(f32[3,1,64,256]{3,2,1,0:T(8,128)S(1)} %get-tuple-element.670), channel_id=1, source_target_pairs={{1,0},{2,1},{3,2},{4,3},{5,4},{6,5},{7,6},{8,7},{9,8},{10,9},{11,1... | collective-permute-start | bytes 589832 | tf_op jit(solution)/shard_map/while/body/eval_jaxpr/while/body/eval_jaxpr/ppermute | solution.py:25
  356.9 12.7 %collective-permute-start.7 = (f32[3,1,64,256]{3,2,1,0:T(8,128)S(1)}, f32[3,1,64,256]{3,2,1,0:T(8,128)S(1)}, u32[]{:S(2)}, u32[]{:S(2)}) collective-permute-start(f32[3,1,64,256]{3,2,1,0:T(8,128)S(1)} %get-tuple-element.671), channel_id=1, source_target_pairs={{0,1},{1,2},{2,3},{3,4},{4,5},{5,6},{6,7},{7,8},{8,9},{9,10},{10,1... | collective-permute-start | bytes 589832 | tf_op jit(solution)/shard_map/while/body/eval_jaxpr/while/body/eval_jaxpr/ppermute | solution.py:22
  373.0 7.6 %collective-permute-start.6 = (f32[3,1,64,256]{3,2,1,0:T(8,128)S(1)}, f32[3,1,64,256]{3,2,1,0:T(8,128)S(1)}, u32[]{:S(2)}, u32[]{:S(2)}) collective-permute-start(f32[3,1,64,256]{3,2,1,0:T(8,128)S(1)} %get-tuple-element.670), channel_id=1, source_target_pairs={{1,0},{2,1},{3,2},{4,3},{5,4},{6,5},{7,6},{8,7},{9,8},{10,9},{11,1... | collective-permute-start | bytes 589832 | tf_op jit(solution)/shard_map/while/body/eval_jaxpr/while/body/eval_jaxpr/ppermute | solution.py:25
  375.0 12.8 %collective-permute-start.7 = (f32[3,1,64,256]{3,2,1,0:T(8,128)S(1)}, f32[3,1,64,256]{3,2,1,0:T(8,128)S(1)}, u32[]{:S(2)}, u32[]{:S(2)}) collective-permute-start(f32[3,1,64,256]{3,2,1,0:T(8,128)S(1)} %get-tuple-element.671), channel_id=1, source_target_pairs={{0,1},{1,2},{2,3},{3,4},{4,5},{5,6},{6,7},{7,8},{8,9},{9,10},{10,1... | collective-permute-start | bytes 589832 | tf_op jit(solution)/shard_map/while/body/eval_jaxpr/while/body/eval_jaxpr/ppermute | solution.py:22
  393.3 16.0 %collective-permute-start.8 = (f32[6,2,64,256]{3,2,1,0:T(8,128)}, f32[6,2,64,256]{3,2,1,0:T(8,128)S(1)}, u32[]{:S(2)}, u32[]{:S(2)}) collective-permute-start(f32[6,2,64,256]{3,2,1,0:T(8,128)} %add.3322), channel_id=1, source_target_pairs={{0,64},{64,128},{128,192},{192,256},{256,320},{320,384},{384,448},... | collective-permute-start | bytes 2359304 | tf_op jit(solution)/shard_map/while/body/eval_jaxpr/ppermute | solution.py:33
  409.5 7.6 %collective-permute-start.6 = (f32[3,1,64,256]{3,2,1,0:T(8,128)S(1)}, f32[3,1,64,256]{3,2,1,0:T(8,128)S(1)}, u32[]{:S(2)}, u32[]{:S(2)}) collective-permute-start(f32[3,1,64,256]{3,2,1,0:T(8,128)S(1)} %get-tuple-element.670), channel_id=1, source_target_pairs={{1,0},{2,1},{3,2},{4,3},{5,4},{6,5},{7,6},{8,7},{9,8},{10,9},{11,1... | collective-permute-start | bytes 589832 | tf_op jit(solution)/shard_map/while/body/eval_jaxpr/while/body/eval_jaxpr/ppermute | solution.py:25
  411.4 11.8 %collective-permute-start.7 = (f32[3,1,64,256]{3,2,1,0:T(8,128)S(1)}, f32[3,1,64,256]{3,2,1,0:T(8,128)S(1)}, u32[]{:S(2)}, u32[]{:S(2)}) collective-permute-start(f32[3,1,64,256]{3,2,1,0:T(8,128)S(1)} %get-tuple-element.671), channel_id=1, source_target_pairs={{0,1},{1,2},{2,3},{3,4},{4,5},{5,6},{6,7},{7,8},{8,9},{9,10},{10,1... | collective-permute-start | bytes 589832 | tf_op jit(solution)/shard_map/while/body/eval_jaxpr/while/body/eval_jaxpr/ppermute | solution.py:22
  428.5 13.9 %collective-permute-start.7 = (f32[3,1,64,256]{3,2,1,0:T(8,128)S(1)}, f32[3,1,64,256]{3,2,1,0:T(8,128)S(1)}, u32[]{:S(2)}, u32[]{:S(2)}) collective-permute-start(f32[3,1,64,256]{3,2,1,0:T(8,128)S(1)} %get-tuple-element.671), channel_id=1, source_target_pairs={{0,1},{1,2},{2,3},{3,4},{4,5},{5,6},{6,7},{7,8},{8,9},{9,10},{10,1... | collective-permute-start | bytes 589832 | tf_op jit(solution)/shard_map/while/body/eval_jaxpr/while/body/eval_jaxpr/ppermute | solution.py:22
  448.0 15.6 %collective-permute-start.8 = (f32[6,2,64,256]{3,2,1,0:T(8,128)}, f32[6,2,64,256]{3,2,1,0:T(8,128)S(1)}, u32[]{:S(2)}, u32[]{:S(2)}) collective-permute-start(f32[6,2,64,256]{3,2,1,0:T(8,128)} %add.3322), channel_id=1, source_target_pairs={{0,64},{64,128},{128,192},{192,256},{256,320},{320,384},{384,448},... | collective-permute-start | bytes 2359304 | tf_op jit(solution)/shard_map/while/body/eval_jaxpr/ppermute | solution.py:33
  465.7 11.8 %collective-permute-start.7 = (f32[3,1,64,256]{3,2,1,0:T(8,128)S(1)}, f32[3,1,64,256]{3,2,1,0:T(8,128)S(1)}, u32[]{:S(2)}, u32[]{:S(2)}) collective-permute-start(f32[3,1,64,256]{3,2,1,0:T(8,128)S(1)} %get-tuple-element.671), channel_id=1, source_target_pairs={{0,1},{1,2},{2,3},{3,4},{4,5},{5,6},{6,7},{7,8},{8,9},{9,10},{10,1... | collective-permute-start | bytes 589832 | tf_op jit(solution)/shard_map/while/body/eval_jaxpr/while/body/eval_jaxpr/ppermute | solution.py:22
  480.9 7.6 %collective-permute-start.6 = (f32[3,1,64,256]{3,2,1,0:T(8,128)S(1)}, f32[3,1,64,256]{3,2,1,0:T(8,128)S(1)}, u32[]{:S(2)}, u32[]{:S(2)}) collective-permute-start(f32[3,1,64,256]{3,2,1,0:T(8,128)S(1)} %get-tuple-element.670), channel_id=1, source_target_pairs={{1,0},{2,1},{3,2},{4,3},{5,4},{6,5},{7,6},{8,7},{9,8},{10,9},{11,1... | collective-permute-start | bytes 589832 | tf_op jit(solution)/shard_map/while/body/eval_jaxpr/while/body/eval_jaxpr/ppermute | solution.py:25
  482.9 13.9 %collective-permute-start.7 = (f32[3,1,64,256]{3,2,1,0:T(8,128)S(1)}, f32[3,1,64,256]{3,2,1,0:T(8,128)S(1)}, u32[]{:S(2)}, u32[]{:S(2)}) collective-permute-start(f32[3,1,64,256]{3,2,1,0:T(8,128)S(1)} %get-tuple-element.671), channel_id=1, source_target_pairs={{0,1},{1,2},{2,3},{3,4},{4,5},{5,6},{6,7},{7,8},{8,9},{9,10},{10,1... | collective-permute-start | bytes 589832 | tf_op jit(solution)/shard_map/while/body/eval_jaxpr/while/body/eval_jaxpr/ppermute | solution.py:22
  502.3 15.6 %collective-permute-start.8 = (f32[6,2,64,256]{3,2,1,0:T(8,128)}, f32[6,2,64,256]{3,2,1,0:T(8,128)S(1)}, u32[]{:S(2)}, u32[]{:S(2)}) collective-permute-start(f32[6,2,64,256]{3,2,1,0:T(8,128)} %add.3322), channel_id=1, source_target_pairs={{0,64},{64,128},{128,192},{192,256},{256,320},{320,384},{384,448},... | collective-permute-start | bytes 2359304 | tf_op jit(solution)/shard_map/while/body/eval_jaxpr/ppermute | solution.py:33
  518.1 7.7 %collective-permute-start.4 = (f32[3,1,64,256]{3,2,1,0:T(8,128)S(1)}, f32[3,1,64,256]{3,2,1,0:T(8,128)S(1)}, u32[]{:S(2)}, u32[]{:S(2)}) collective-permute-start(f32[3,1,64,256]{3,2,1,0:T(8,128)S(1)} %get-tuple-element.661), channel_id=1, source_target_pairs={{1,0},{2,1},{3,2},{4,3},{5,4},{6,5},{7,6},{8,7},{9,8},{10,9},{11,1... | collective-permute-start | bytes 589832 | tf_op jit(solution)/shard_map/while/body/eval_jaxpr/ppermute | solution.py:25
  520.2 11.8 %collective-permute-start.5 = (f32[3,1,64,256]{3,2,1,0:T(8,128)S(1)}, f32[3,1,64,256]{3,2,1,0:T(8,128)S(1)}, u32[]{:S(2)}, u32[]{:S(2)}) collective-permute-start(f32[3,1,64,256]{3,2,1,0:T(8,128)S(1)} %get-tuple-element.662), channel_id=1, source_target_pairs={{0,1},{1,2},{2,3},{3,4},{4,5},{5,6},{6,7},{7,8},{8,9},{9,10},{10,1... | collective-permute-start | bytes 589832 | tf_op jit(solution)/shard_map/while/body/eval_jaxpr/ppermute | solution.py:22
  537.3 11.8 %collective-permute-start.5 = (f32[3,1,64,256]{3,2,1,0:T(8,128)S(1)}, f32[3,1,64,256]{3,2,1,0:T(8,128)S(1)}, u32[]{:S(2)}, u32[]{:S(2)}) collective-permute-start(f32[3,1,64,256]{3,2,1,0:T(8,128)S(1)} %get-tuple-element.662), channel_id=1, source_target_pairs={{0,1},{1,2},{2,3},{3,4},{4,5},{5,6},{6,7},{7,8},{8,9},{9,10},{10,1... | collective-permute-start | bytes 589832 | tf_op jit(solution)/shard_map/while/body/eval_jaxpr/ppermute | solution.py:22
  (5 other events, 63.1 us)
where the time goes:
time: 556 us; the launch traced here: 554 us
  waiting for transfers between devices  297 us (53%)
  starting transfers between devices  149 us (27%)
  other arithmetic  103 us (19%)
    ppermute x22, waiting for transfers between devices, padded_2(): lax.ppermute(lax.slice_in_dim(block, block.shape[dim] - width, None, axis...  145 us
    ppermute x7, waiting for transfers between devices, passed_along(): return lax.ppermute(block, axis, route)  113 us
    ppermute x22, starting transfers between devices, padded_2(): lax.ppermute(lax.slice_in_dim(block, block.shape[dim] - width, None, axis...  87.7 us
    ppermute x22, starting transfers between devices, padded_2(): lax.ppermute(lax.slice_in_dim(block, 0, width, axis=dim), axis, backward)  48 us
    add x22, other arithmetic, advance(): displaced = displaced + time_step * velocity  45.9 us
    ppermute x22, waiting for transfers between devices, padded_2(): lax.ppermute(lax.slice_in_dim(block, 0, width, axis=dim), axis, backward)  38.8 us
    add x66, other arithmetic, acceleration(): along = along + 0.25 * (both_up - up_down - down_up + both_down)  20.8 us
    add x7, other arithmetic, link(): propagate(current, COARSE, DT_COARSE, stiff_shear, stiff_bulk, loading, s...  15 us
  transfers between devices with their start and end apart: 51, of which 51 were waited for; matrix products, arithmetic and copies ran while one was open for 0% of the time, Pallas kernels for 0%

commit v1 on v0

v1 whole, which is shorter than its diff:
```python
import jax
import jax.numpy as jnp
from jax import lax
from jax.experimental import pallas as pl
from jax.experimental.pallas import tpu as pltpu
from jax.sharding import PartitionSpec as P

FINE = 4
COARSE = 2
DT_FINE = 0.18
DT_COARSE = 0.36
PAD = 8
ROWS = 16
MESH = pl.DeviceIdType.MESH


def kernel(
    windows,
    slabs,
    states,
    load,
    zones,
    shear_table,
    lame_table,
    amp_table,
    cycle_index,
    out,
    disp,
    halo,
    speed,
    drift,
    arrived,
    shear,
    bulk,
    send_sem,
    recv_sem,
    pass_sem,
):
    win = lax.axis_index("win")
    slab = lax.axis_index("slab")
    ny, nx = states.shape[3], states.shape[4]
    inner = pl.ds(PAD, ny)
    has_low = slab > 0
    has_high = slab < slabs - 1
    has_prev = win > 0
    has_next = win < windows - 1

    edge = jnp.zeros((PAD, nx), jnp.float32)
    for c in range(3):
        for slot in range(disp.shape[0]):
            for p in range(2):
                disp[slot, c, p, pl.ds(0, PAD), :] = edge
                disp[slot, c, p, pl.ds(PAD + ny, PAD), :] = edge
        for slot in range(halo.shape[0]):
            for side in range(2):
                halo[slot, side, c, pl.ds(0, PAD), :] = edge
                halo[slot, side, c, pl.ds(PAD + ny, PAD), :] = edge
    plane_zero = jnp.zeros((ny, nx), jnp.float32)
    for side, missing in ((0, slab == 0), (1, slab == slabs - 1)):

        @pl.when(missing)
        def _(side=side):
            for slot in range(halo.shape[0]):
                for c in range(3):
                    halo[slot, side, c, inner, :] = plane_zero

    barrier = pltpu.get_barrier_semaphore()
    for present, target in (
        (has_low, {"slab": slab - 1}),
        (has_high, {"slab": slab + 1}),
        (has_prev, {"win": win - 1}),
        (has_next, {"win": win + 1}),
    ):

        @pl.when(present)
        def _(target=target):
            pl.semaphore_signal(barrier, inc=1, device_id=target, device_id_type=MESH)

    expected = (
        has_low.astype(jnp.int32)
        + has_high.astype(jnp.int32)
        + has_prev.astype(jnp.int32)
        + has_next.astype(jnp.int32)
    )
    pl.semaphore_wait(barrier, expected)

    def halo_copy(source, slot, p):
        return pltpu.make_async_remote_copy(
            src_ref=source,
            dst_ref=halo.at[slot, 1 - p, :, inner, :],
            send_sem=send_sem.at[slot, p],
            recv_sem=recv_sem.at[slot, 1 - p],
            device_id={"slab": slab - 1 + 2 * p},
            device_id_type=MESH,
        )

    def first_source(p):
        return states.at[0, pl.ds(0, 3), p]

    def disp_source(slot, p):
        return disp.at[slot, :, p, inner, :]

    reach = (has_low, has_high)

    def send_plane(source, slot, p):
        @pl.when(reach[p])
        def _():
            halo_copy(source, slot, p).start()

    def await_halo(slot, side):
        @pl.when(reach[side])
        def _():
            halo_copy(disp_source(0, 1 - side), slot, 1 - side).wait_recv()

    for p in range(2):
        send_plane(first_source(p), 0, p)

    for c in range(3):
        for p in range(2):
            disp[0, c, p, inner, :] = states[0, c, p]
            speed[c, p] = states[0, 3 + c, p]
    ids = zones[...]
    mu = jnp.zeros(ids.shape, jnp.float32)
    lame = jnp.zeros(ids.shape, jnp.float32)
    for k in range(shear_table.shape[0]):
        mu = jnp.where(ids == k, shear_table[k], mu)
        lame = jnp.where(ids == k, lame_table[k], lame)
    shear[...] = mu * (1.0 / 30.0)
    bulk[...] = lame + mu
    amp = amp_table[cycle_index[win]]

    lane = lax.broadcasted_iota(jnp.int32, (ROWS, nx), 1)
    first_lane = lane == 0
    last_lane = lane == nx - 1
    tall = ROWS + 2 * PAD

    def left(f):
        return jnp.where(first_lane, 0.0, pltpu.roll(f, 1, 1))

    def right(f):
        return jnp.where(last_lane, 0.0, pltpu.roll(f, nx - 1, 1))

    def above(f):
        return pltpu.roll(f, 1, 0)[PAD : PAD + ROWS]

    def below(f):
        return pltpu.roll(f, tall - 1, 0)[PAD : PAD + ROWS]

    def core(f):
        return f[PAD : PAD + ROWS]

    def plane_step(slot, hslot, p, h, velocity, loaded, finish):
        def body(block, carry):
            start = pl.multiple_of(block * ROWS, ROWS)
            rows = pl.ds(start, ROWS)
            window = pl.ds(start, tall)
            low, mid, high = [], [], []
            for c in range(3):
                own = [disp[slot, c, q, window, :] for q in range(2)]
                mid.append(own[p])
                low.append(halo[hslot, 0, c, window, :] if p == 0 else own[0])
                high.append(own[1] if p == 0 else halo[hslot, 1, c, window, :])
            zs = [low[c] + high[c] for c in range(3)]
            zd = [high[c] - low[c] for c in range(3)]
            laps = []
            for c in range(3):
                face = 3.0 * zs[c] + 14.0 * mid[c]
                diag = zs[c] + 3.0 * mid[c]
                side = core(face) + above(diag) + below(diag)
                laps.append(
                    14.0 * core(zs[c])
                    - 128.0 * core(mid[c])
                    + (above(face) + below(face))
                    + (left(side) + right(side))
                )
            ux, uy = mid[0], mid[1]
            uy_up, uy_down = below(uy), above(uy)
            cross = (uy_up - uy_down) + core(zd[2])
            ux_core = core(ux)
            ux_left, ux_right = left(ux_core), right(ux_core)
            lead_x = (ux_left + ux_right - 2.0 * ux_core) + 0.25 * (right(cross) - left(cross))
            row_diff = below(ux) - above(ux)
            lead_y = (uy_up + uy_down - 2.0 * core(uy)) + 0.25 * (
                (right(row_diff) - left(row_diff)) + (below(zd[2]) - above(zd[2]))
            )
            zx = core(zd[0])
            lead_z = (core(zs[2]) - 2.0 * core(mid[2])) + 0.25 * (
                (right(zx) - left(zx)) + (below(zd[1]) - above(zd[1]))
            )
            mu_rows = shear[p, rows, :]
            bulk_rows = bulk[p, rows, :]
            for c, lead in enumerate((lead_x, lead_y, lead_z)):
                rate = mu_rows * laps[c] + bulk_rows * lead
                if loaded:
                    rate = rate + amp * load[c, p, rows, :].astype(jnp.float32)
                moved = velocity[c, p, rows, :] + h * rate
                finish(c, p, start, moved, core(mid[c]) + h * moved)
            return carry

        lax.fori_loop(0, ny // ROWS, body, 0)

    def keep(slot, velocity):
        def finish(c, p, start, moved, placed):
            velocity[c, p, pl.ds(start, ROWS), :] = moved
            disp[slot, c, p, pl.ds(start + PAD, ROWS), :] = placed

        return finish

    for step in range(FINE):
        for p in range(2):
            await_halo(step, p)
            plane_step(step, step, p, DT_FINE, speed, True, keep(step + 1, speed))
            if step + 1 < FINE:
                send_plane(disp_source(step + 1, p), step + 1, p)

    pass_on = pltpu.make_async_remote_copy(
        src_ref=out.at[0],
        dst_ref=arrived,
        send_sem=pass_sem.at[0],
        recv_sem=pass_sem.at[1],
        device_id={"win": win + 1},
        device_id_type=MESH,
    )

    @pl.when(win == 0)
    def _():
        for c in range(3):
            for p in range(2):
                out[0, c, p] = disp[FINE, c, p, inner, :]
                out[0, 3 + c, p] = speed[c, p]

    @pl.when(has_prev)
    def _():
        pass_on.wait_recv()
        base = FINE + 1
        for p in range(2):
            for c in range(3):
                disp[base, c, p, inner, :] = arrived[c, p] - states[0, c, p]
            send_plane(disp_source(base, p), FINE, p)
        for p in range(2):
            for c in range(3):
                drift[c, p] = arrived[3 + c, p] - states[0, 3 + c, p]

        def conclude(c, p, start, moved, placed):
            rows = pl.ds(start, ROWS)
            out[0, c, p, rows, :] = disp[FINE, c, p, pl.ds(start + PAD, ROWS), :] + placed
            out[0, 3 + c, p, rows, :] = speed[c, p, rows, :] + moved

        for step in range(COARSE):
            for p in range(2):
                await_halo(FINE + step, p)
                last = step + 1 == COARSE
                finish = conclude if last else keep(base + step + 1, drift)
                plane_step(base + step, FINE + step, p, DT_COARSE, drift, False, finish)
                if not last:
                    send_plane(disp_source(base + step + 1, p), FINE + step + 1, p)

    @pl.when(has_next)
    def _():
        pass_on.start()

    for slot in range(FINE):
        for p in range(2):

            @pl.when(reach[p])
            def _(slot=slot, p=p):
                halo_copy(disp_source(slot, p), slot, p).wait_send()

    for slot in range(FINE, FINE + COARSE):
        for p in range(2):

            @pl.when(jnp.logical_and(reach[p], has_prev))
            def _(slot=slot, p=p):
                halo_copy(disp_source(slot, p), slot, p).wait_send()

    @pl.when(has_next)
    def _():
        pass_on.wait_send()


def solution(mesh):
    windows, slabs = mesh.shape["win"], mesh.shape["slab"]

    def shards(states, load, zones, shear_table, lame_table, amp_table, cycle_index):
        _, _, nz, ny, nx = states.shape
        vmem = pl.BlockSpec(memory_space=pltpu.VMEM)
        smem = pl.BlockSpec(memory_space=pltpu.SMEM)
        f32 = jnp.float32
        steps = FINE + COARSE
        tall = ny + 2 * PAD
        return pl.pallas_call(
            lambda *refs: kernel(windows, slabs, *refs),
            out_shape=jax.ShapeDtypeStruct(states.shape, f32),
            in_specs=[vmem] * 3 + [smem] * 4,
            out_specs=vmem,
            scratch_shapes=[
                pltpu.VMEM((steps + 1, 3, nz, tall, nx), f32),
                pltpu.VMEM((steps, 2, 3, tall, nx), f32),
                pltpu.VMEM((3, nz, ny, nx), f32),
                pltpu.VMEM((3, nz, ny, nx), f32),
                pltpu.VMEM((6, nz, ny, nx), f32),
                pltpu.VMEM((nz, ny, nx), f32),
                pltpu.VMEM((nz, ny, nx), f32),
                pltpu.SemaphoreType.DMA((steps, 2)),
                pltpu.SemaphoreType.DMA((steps, 2)),
                pltpu.SemaphoreType.DMA((2,)),
            ],
            compiler_params=pltpu.CompilerParams(
                collective_id=0, has_side_effects=True, vmem_limit_bytes=48 * 2**20
            ),
            name="parareal",
        )(states, load, zones, shear_table, lame_table, amp_table, cycle_index)

    placed = (
        P("win", None, "slab", None, None),
        P(None, "slab", None, None),
        P("slab", None, None),
        P(),
        P(),
        P(),
        P(),
    )
    return jax.shard_map(
        shards,
        mesh=mesh,
        in_specs=placed,
        out_specs=P("win", None, "slab", None, None),
        check_vma=False,
    )
```

time: 556 us -> 181 us (0.33)
  the two profiles are of different devices: /device:TPU:320 before, /device:TPU:449 now
where the time goes in v1:
time: 181 us
  Pallas kernels  175 us (97%)
  local copies, waits for them, and re-layouts  6.46 us (4%)
    pallas_call x1, Pallas kernels, shards(): pl.pallas_call(lambda *refs: kernel(windows, slabs, *refs), out_shape=jax...  175 us
    unnamed x15, local copies, waits for them, and re-layouts  6.46 us

profile of v1, /device:TPU:449, one launch (start us, length us, event | category | flops | bytes accessed | tf_op | source)
XLA Modules:
  0.0 181.1 jit_solution(4991407233309123182)
XLA Ops:
  0.0 0.0 copy-start
  0.0 1.1 copy-done
  1.1 0.0 copy-start.1
  1.1 0.9 copy-done.1
  2.1 0.0 copy-start.2
  2.1 0.9 copy-done.2
  3.0 0.0 copy-start.3
  3.0 0.7 copy-done.3
  3.6 0.0 copy-start.4
  3.6 0.7 copy-done.4
  4.3 0.0 copy-start.5
  4.3 0.7 copy-done.5
  4.9 0.0 copy-start.6
  4.9 0.7 copy-done.6
  5.6 174.6 %parareal.1 = f32[1,6,2,64,256]{4,3,2,1,0:T(8,128)S(1)} custom-call(f32[1,6,2,64,256]{4,3,2,1,0:T(8,128)S(1)} %copy-done, bf16[3,2,64,256]{3,2,1,0:T(8,128)(2,1)S(1)} %copy-done.1, s32[2,64,256]{2,1,0:T(8,128)S(1)} %copy-done.2, f32[8]{0:T(128)S(1)} %copy-done.3, f32[8]{0:T(128)S(1)} %copy-done.4, f32[16]{0:T(128)S(1)} %copy-done.5, s32[16]{0:T(128)S(1)} %copy-done.6), custom_call_target="tpu_custom_call" | custom-call | tf_op jit(solution)/shard_map/parareal/pallas_call | solution.py:291
  180.2 0.9 copy.9
Async XLA Ops:
  0.0 1.1 copy-start
  1.1 0.9 copy-start.1
  2.1 0.9 copy-start.2
  3.0 0.7 copy-start.3
  3.6 0.7 copy-start.4
  4.3 0.7 copy-start.5
  4.9 0.7 copy-start.6

commit v2 on v1

v2 whole, which is shorter than its diff:
```python
import jax
import jax.numpy as jnp
from jax import lax
from jax.experimental import pallas as pl
from jax.experimental.pallas import tpu as pltpu
from jax.sharding import PartitionSpec as P

FINE = 4
DT_FINE = 0.18
DT_COARSE = 0.36
PAD = 8
ROWS = 16
MESH = pl.DeviceIdType.MESH


def stencil(low, mid, high, trim):
    tall, nx = mid[0].shape
    size = tall - 2 * trim
    lane = lax.broadcasted_iota(jnp.int32, (size, nx), 1)
    first_lane = lane == 0
    last_lane = lane == nx - 1

    def left(f):
        return jnp.where(first_lane, 0.0, pltpu.roll(f, 1, 1))

    def right(f):
        return jnp.where(last_lane, 0.0, pltpu.roll(f, nx - 1, 1))

    def core(f):
        return f[trim : trim + size]

    def above(f):
        return core(pltpu.roll(f, 1, 0))

    def below(f):
        return core(pltpu.roll(f, tall - 1, 0))

    zs = [low[c] + high[c] for c in range(3)]
    zd = [high[c] - low[c] for c in range(3)]
    laps = []
    for c in range(3):
        face = 3.0 * zs[c] + 14.0 * mid[c]
        diag = zs[c] + 3.0 * mid[c]
        side = core(face) + above(diag) + below(diag)
        laps.append(
            14.0 * core(zs[c])
            - 128.0 * core(mid[c])
            + (above(face) + below(face))
            + (left(side) + right(side))
        )
    ux, uy = mid[0], mid[1]
    uy_up, uy_down = below(uy), above(uy)
    cross = (uy_up - uy_down) + core(zd[2])
    ux_core = core(ux)
    lead_x = (left(ux_core) + right(ux_core) - 2.0 * ux_core) + 0.25 * (right(cross) - left(cross))
    row_diff = below(ux) - above(ux)
    lead_y = (uy_up + uy_down - 2.0 * core(uy)) + 0.25 * (
        (right(row_diff) - left(row_diff)) + (below(zd[2]) - above(zd[2]))
    )
    zx = core(zd[0])
    lead_z = (core(zs[2]) - 2.0 * core(mid[2])) + 0.25 * (
        (right(zx) - left(zx)) + (below(zd[1]) - above(zd[1]))
    )
    return laps, (lead_x, lead_y, lead_z)


def kernel(
    windows,
    slabs,
    states_hbm,
    load_hbm,
    zones_hbm,
    shear_hbm,
    lame_hbm,
    amp_hbm,
    cycle_hbm,
    out,
    states,
    load,
    zones,
    shear_table,
    lame_table,
    amp_table,
    cycle_index,
    disp,
    halo,
    speed,
    fine_end,
    next_zones,
    shear,
    bulk,
    starts,
    fines,
    ends,
    wide_disp,
    wide_speed,
    mid_disp,
    mid_speed,
    rim_out,
    rim_in,
    load_sem,
    zone_send,
    zone_recv,
    halo_send,
    halo_recv,
    start_send,
    start_recv,
    fine_send,
    fine_recv,
    home_send,
    home_recv,
    wide_send,
    wide_recv,
):
    win = lax.axis_index("win")
    slab = lax.axis_index("slab")
    ny, nx = states.shape[2], states.shape[3]
    part = ny // windows
    wide = part + 2 * PAD
    inner = pl.ds(PAD, ny)
    own_rows = pl.ds(pl.multiple_of(win * part, 8), part)
    has_slab = (slab > 0, slab < slabs - 1)
    has_win = (win > 0, win < windows - 1)

    pairs = (
        (states_hbm.at[0], states),
        (zones_hbm, zones),
        (load_hbm, load),
        (shear_hbm, shear_table),
        (lame_hbm, lame_table),
        (amp_hbm, amp_table),
        (cycle_hbm, cycle_index),
    )
    loads = [pltpu.make_async_copy(a, b, load_sem.at[k]) for k, (a, b) in enumerate(pairs)]
    for copy in loads:
        copy.start()

    around = [(a, b) for a in (-1, 0, 1) for b in (-1, 0, 1) if (a, b) != (0, 0)]

    def present(step):
        a, b = step
        found = None
        if a:
            found = has_slab[(a + 1) // 2]
        if b:
            side = has_win[(b + 1) // 2]
            found = side if found is None else jnp.logical_and(found, side)
        return found

    barrier = pltpu.get_barrier_semaphore()
    expected = jnp.int32(windows - 1)
    for k in range(1, windows):
        target = {"win": lax.rem(win + k, windows)}
        pl.semaphore_signal(barrier, inc=1, device_id=target, device_id_type=MESH)
    for a, b in around:
        if a:
            there = present((a, b))
            expected = expected + there.astype(jnp.int32)

            @pl.when(there)
            def _(a=a, b=b):
                target = {"win": win + b, "slab": slab + a}
                pl.semaphore_signal(barrier, inc=1, device_id=target, device_id_type=MESH)

    edge = jnp.zeros((PAD, nx), jnp.float32)
    for c in range(3):
        for slot in range(disp.shape[0]):
            for p in range(2):
                disp[slot, c, p, pl.ds(0, PAD), :] = edge
                disp[slot, c, p, pl.ds(PAD + ny, PAD), :] = edge
        for slot in range(halo.shape[0]):
            for side in range(2):
                halo[slot, side, c, pl.ds(0, PAD), :] = edge
                halo[slot, side, c, pl.ds(PAD + ny, PAD), :] = edge
    plane_zero = jnp.zeros((ny, nx), jnp.float32)
    for side in range(2):

        @pl.when(jnp.logical_not(has_slab[side]))
        def _(side=side):
            for slot in range(halo.shape[0]):
                for c in range(3):
                    halo[slot, side, c, inner, :] = plane_zero

    def clear(n, carry):
        for c in range(3):
            wide_disp[n, c] = jnp.zeros(wide_disp.shape[2:], jnp.float32)
            wide_speed[n, c] = jnp.zeros(wide_speed.shape[2:], jnp.float32)
        return carry

    lax.fori_loop(0, wide_disp.shape[0], clear, 0)
    tall_zero = jnp.zeros(shear.shape[1:], jnp.float32)
    for q in range(4):
        shear[q] = tall_zero
        bulk[q] = tall_zero

    pl.semaphore_wait(barrier, expected)

    def halo_copy(source, slot, p):
        return pltpu.make_async_remote_copy(
            src_ref=source,
            dst_ref=halo.at[slot, 1 - p, :, inner, :],
            send_sem=halo_send.at[slot, p],
            recv_sem=halo_recv.at[slot, 1 - p],
            device_id={"slab": slab - 1 + 2 * p},
            device_id_type=MESH,
        )

    def disp_source(slot, p):
        return disp.at[slot, :, p, inner, :]

    def send_plane(source, slot, p):
        @pl.when(has_slab[p])
        def _():
            halo_copy(source, slot, p).start()

    def await_halo(slot, side):
        @pl.when(has_slab[side])
        def _():
            halo_copy(disp_source(0, 1 - side), slot, 1 - side).wait_recv()

    def zone_copy(p):
        return pltpu.make_async_remote_copy(
            src_ref=zones.at[p],
            dst_ref=next_zones.at[1 - p],
            send_sem=zone_send.at[p],
            recv_sem=zone_recv.at[1 - p],
            device_id={"slab": slab - 1 + 2 * p},
            device_id_type=MESH,
        )

    def share(source, target, send, recv, k):
        other = lax.rem(win + k, windows)
        return pltpu.make_async_remote_copy(
            src_ref=source.at[:, :, pl.ds(pl.multiple_of(other * part, 8), part), :],
            dst_ref=target.at[win],
            send_sem=send.at[k],
            recv_sem=recv.at[win],
            device_id={"win": other},
            device_id_type=MESH,
        )

    def shared(target, recv, n):
        return pltpu.make_async_remote_copy(
            src_ref=target.at[n],
            dst_ref=target.at[n],
            send_sem=recv.at[n],
            recv_sem=recv.at[n],
            device_id={"win": lax.rem(win + 1, windows)},
            device_id_type=MESH,
        )

    loads[0].wait()
    for p in range(2):
        send_plane(states.at[pl.ds(0, 3), p], 0, p)
    loads[1].wait()
    for p in range(2):

        @pl.when(has_slab[p])
        def _(p=p):
            zone_copy(p).start()

    for k in range(1, windows):
        share(states, starts, start_send, start_recv, k).start()

    for c in range(3):
        for p in range(2):
            disp[0, c, p, inner, :] = states[c, p]
            speed[c, p] = states[3 + c, p]
    for copy in loads[2:]:
        copy.wait()

    def material(ids, q):
        mu = jnp.zeros(ids.shape, jnp.float32)
        lame = jnp.zeros(ids.shape, jnp.float32)
        for k in range(shear_table.shape[0]):
            mu = jnp.where(ids == k, shear_table[k], mu)
            lame = jnp.where(ids == k, lame_table[k], lame)
        shear[q, inner, :] = mu * (1.0 / 30.0)
        bulk[q, inner, :] = lame + mu

    for p in range(2):
        material(zones[p], 1 + p)
    amp = amp_table[cycle_index[win]]

    for step in range(FINE):
        for p in range(2):
            await_halo(step, p)

            def body(block, carry, step=step, p=p):
                start = pl.multiple_of(block * ROWS, ROWS)
                rows = pl.ds(start, ROWS)
                shifted = pl.ds(start + PAD, ROWS)
                window = pl.ds(start, ROWS + 2 * PAD)
                low, mid, high = [], [], []
                for c in range(3):
                    own = [disp[step, c, q, window, :] for q in range(2)]
                    mid.append(own[p])
                    low.append(halo[step, 0, c, window, :] if p == 0 else own[0])
                    high.append(own[1] if p == 0 else halo[step, 1, c, window, :])
                laps, leads = stencil(low, mid, high, PAD)
                mu = shear[1 + p, shifted, :]
                stiff = bulk[1 + p, shifted, :]
                for c in range(3):
                    rate = mu * laps[c] + stiff * leads[c]
                    rate = rate + amp * load[c, p, rows, :].astype(jnp.float32)
                    moved = speed[c, p, rows, :] + DT_FINE * rate
                    placed = mid[c][PAD : PAD + ROWS] + DT_FINE * moved
                    if step + 1 < FINE:
                        speed[c, p, rows, :] = moved
                        disp[step + 1, c, p, shifted, :] = placed
                    else:
                        fine_end[c, p, rows, :] = placed
                        fine_end[3 + c, p, rows, :] = moved
                return carry

            lax.fori_loop(0, ny // ROWS, body, 0)
            if step + 1 < FINE:
                send_plane(disp_source(step + 1, p), step + 1, p)

    for k in range(1, windows):
        share(fine_end, fines, fine_send, fine_recv, k).start()
    fines[win] = fine_end[:, :, own_rows, :]
    starts[win] = states[:, :, own_rows, :]

    @pl.when(win == 0)
    def _():
        out[0] = fine_end[...]

    for side in range(2):

        @pl.when(has_slab[side])
        def _(side=side):
            zone_copy(1 - side).wait_recv()
            material(next_zones[side], 3 * side)

    centre = pl.ds(PAD, part)
    deep = 2

    def wide_copies(n, step):
        a, b = step
        which = around.index(step)
        if b == 0:
            sources = (wide_disp.at[n, :, pl.ds(2, 2), centre, :],)
            sources += (wide_speed.at[n, :, pl.ds(1 + (a + 1) // 2, 1), centre, :],)
            targets = (wide_disp.at[n, :, pl.ds(2 - 2 * a, 2), centre, :],)
            targets += (wide_speed.at[n, :, pl.ds(0 if a > 0 else 3, 1), centre, :],)
        else:
            planes = pl.ds(0, 2) if a == 0 else pl.ds((a + 1) // 2, 1)
            mirror = around.index((-a, -b))
            edge_rows = rim_out.at[n, (b + 1) // 2]
            landing = rim_in.at[n, mirror]
            sources = (edge_rows.at[pl.ds(0, 3)], edge_rows.at[pl.ds(3, 3), planes])
            targets = (landing.at[pl.ds(0, 3)], landing.at[pl.ds(3, 3), planes])
        came = around.index((-a, -b))
        return [
            pltpu.make_async_remote_copy(
                src_ref=source,
                dst_ref=target,
                send_sem=wide_send.at[n, which, k],
                recv_sem=wide_recv.at[n, came, k],
                device_id={"win": win + b, "slab": slab + a},
                device_id_type=MESH,
            )
            for k, (source, target) in enumerate(zip(sources, targets))
        ]

    def turn(n, carry):
        @pl.when(jnp.logical_and(n == 1, win != 0))
        def _():
            shared(fines, fine_recv, 0).wait_recv()

        @pl.when(n != win)
        def _():
            shared(starts, start_recv, n).wait_recv()

        previous = ends.at[n - 1]

        @pl.when(n == 1)
        def _():
            ends[0] = fines[0]

        for c in range(3):
            for p in range(2):
                gap = previous[c, p] - starts[n, c, p]
                gap_speed = previous[3 + c, p] - starts[n, 3 + c, p]
                wide_disp[n, c, 2 + p, centre, :] = gap
                wide_speed[n, c, 1 + p, centre, :] = gap_speed
                for side in range(2):
                    first = (part - deep) * side
                    rim_out[n, side, c, p] = gap[first : first + deep]
                    rim_out[n, side, 3 + c, p] = gap_speed[first : first + deep]
        for step in around:

            @pl.when(present(step))
            def _(step=step):
                for copy in wide_copies(n, step):
                    copy.start()

        for step in around:

            @pl.when(present(step))
            def _(step=step):
                a, b = step
                for copy in wide_copies(n, (-a, -b)):
                    copy.wait_recv()
                if b:
                    which = around.index(step)
                    rows = pl.ds(PAD - deep if b < 0 else PAD + part, deep)
                    for c in range(3):
                        for p in range(2):
                            wide_disp[n, c, 2 + 2 * a + p, rows, :] = rim_in[n, which, c, p]
                        for p in range(2) if a == 0 else ((1 if a < 0 else 0),):
                            q = 1 + 2 * a + p
                            wide_speed[n, c, q, rows, :] = rim_in[n, which, 3 + c, p]

        rows = pl.ds(pl.multiple_of(win * part, 8), wide)
        for q in range(4):
            planes = [[wide_disp[n, c, q + k] for c in range(3)] for k in range(3)]
            laps, leads = stencil(*planes, 0)
            mu = shear[q, rows, :]
            stiff = bulk[q, rows, :]
            for c in range(3):
                rate = mu * laps[c] + stiff * leads[c]
                moved = wide_speed[n, c, q] + DT_COARSE * rate
                mid_disp[c, q] = planes[1][c] + DT_COARSE * moved
                if q in (1, 2):
                    mid_speed[c, q - 1] = moved[PAD : PAD + part]

        @pl.when(n != win)
        def _():
            shared(fines, fine_recv, n).wait_recv()

        rows = pl.ds(pl.multiple_of(win * part + PAD, 8), part)
        for p in range(2):
            planes = [[mid_disp[c, p + k] for c in range(3)] for k in range(3)]
            laps, leads = stencil(*planes, PAD)
            mu = shear[1 + p, rows, :]
            stiff = bulk[1 + p, rows, :]
            for c in range(3):
                rate = mu * laps[c] + stiff * leads[c]
                moved = mid_speed[c, p] + DT_COARSE * rate
                placed = planes[1][c][PAD : PAD + part] + DT_COARSE * moved
                ends[n, c, p] = fines[n, c, p] + placed
                ends[n, 3 + c, p] = fines[n, 3 + c, p] + moved

        @pl.when(n == win)
        def _():
            out[0, :, :, own_rows, :] = ends[n]

        @pl.when(n != win)
        def _():
            home(n).start()

        for step in around:

            @pl.when(present(step))
            def _(step=step):
                for copy in wide_copies(n, step):
                    copy.wait_send()

        return carry

    def home(n):
        return pltpu.make_async_remote_copy(
            src_ref=ends.at[n],
            dst_ref=out.at[0, :, :, own_rows, :],
            send_sem=home_send.at[n],
            recv_sem=home_recv.at[win],
            device_id={"win": n},
            device_id_type=MESH,
        )

    lax.fori_loop(1, windows, turn, 0)

    for n in range(windows):

        @pl.when(n != win)
        def _(n=n):
            if n == 0:
                shared(starts, start_recv, 0).wait_recv()
            else:
                home(n).wait_send()

        @pl.when(jnp.logical_and(win != 0, n != win))
        def _(n=n):
            rows = pl.ds(n * part, part)
            pltpu.make_async_remote_copy(
                src_ref=ends.at[0],
                dst_ref=out.at[0, :, :, rows, :],
                send_sem=home_send.at[0],
                recv_sem=home_recv.at[n],
                device_id={"win": lax.rem(win + 1, windows)},
                device_id_type=MESH,
            ).wait_recv()

    for k in range(1, windows):
        share(states, starts, start_send, start_recv, k).wait_send()
        share(fine_end, fines, fine_send, fine_recv, k).wait_send()
    for p in range(2):

        @pl.when(has_slab[p])
        def _(p=p):
            zone_copy(p).wait_send()
            for slot in range(FINE):
                halo_copy(disp_source(slot, p), slot, p).wait_send()


def solution(mesh):
    windows, slabs = mesh.shape["win"], mesh.shape["slab"]

    def shards(states, load, zones, shear_table, lame_table, amp_table, cycle_index):
        _, _, nz, ny, nx = states.shape
        f32 = jnp.float32
        tall = ny + 2 * PAD
        part = ny // windows
        wide = part + 2 * PAD
        dma = pltpu.SemaphoreType.DMA
        return pl.pallas_call(
            lambda *refs: kernel(windows, slabs, *refs),
            out_shape=jax.ShapeDtypeStruct(states.shape, f32),
            in_specs=[pl.BlockSpec(memory_space=pl.ANY)] * 7,
            out_specs=pl.BlockSpec(memory_space=pltpu.VMEM),
            scratch_shapes=[
                pltpu.VMEM(states.shape[1:], f32),
                pltpu.VMEM(load.shape, load.dtype),
                pltpu.VMEM(zones.shape, jnp.int32),
                pltpu.SMEM(shear_table.shape, f32),
                pltpu.SMEM(lame_table.shape, f32),
                pltpu.SMEM(amp_table.shape, f32),
                pltpu.SMEM(cycle_index.shape, jnp.int32),
                pltpu.VMEM((FINE, 3, nz, tall, nx), f32),
                pltpu.VMEM((FINE, 2, 3, tall, nx), f32),
                pltpu.VMEM((3, nz, ny, nx), f32),
                pltpu.VMEM((6, nz, ny, nx), f32),
                pltpu.VMEM((2, ny, nx), jnp.int32),
                pltpu.VMEM((4, tall, nx), f32),
                pltpu.VMEM((4, tall, nx), f32),
                pltpu.VMEM((windows, 6, nz, part, nx), f32),
                pltpu.VMEM((windows, 6, nz, part, nx), f32),
                pltpu.VMEM((windows, 6, nz, part, nx), f32),
                pltpu.VMEM((windows, 3, 6, wide, nx), f32),
                pltpu.VMEM((windows, 3, 4, wide, nx), f32),
                pltpu.VMEM((3, 4, wide, nx), f32),
                pltpu.VMEM((3, 2, part, nx), f32),
                pltpu.VMEM((windows, 2, 6, 2, 2, nx), f32),
                pltpu.VMEM((windows, 8, 6, 2, 2, nx), f32),
                dma((7,)),
                dma((2,)),
                dma((2,)),
                dma((FINE, 2)),
                dma((FINE, 2)),
                dma((windows,)),
                dma((windows,)),
                dma((windows,)),
                dma((windows,)),
                dma((windows,)),
                dma((windows,)),
                dma((windows, 8, 2)),
                dma((windows, 8, 2)),
            ],
            compiler_params=pltpu.CompilerParams(
                collective_id=0, has_side_effects=True, vmem_limit_bytes=60 * 2**20
            ),
            name="parareal",
        )(states, load, zones, shear_table, lame_table, amp_table, cycle_index)

    placed = (
        P("win", None, "slab", None, None),
        P(None, "slab", None, None),
        P("slab", None, None),
        P(),
        P(),
        P(),
        P(),
    )
    return jax.shard_map(
        shards,
        mesh=mesh,
        in_specs=placed,
        out_specs=P("win", None, "slab", None, None),
        check_vma=False,
    )
```

time: 181 us -> 126 us (0.70)
  the two profiles are of different devices: /device:TPU:449 before, /device:TPU:451 now
where the time goes in v2:
time: 126 us
  Pallas kernels  124 us (98%)
  local copies, waits for them, and re-layouts  2.06 us (2%)
    pallas_call x1, Pallas kernels, shards(): pl.pallas_call(lambda *refs: kernel(windows, slabs, *refs), out_shape=jax...  124 us

profile of v2, /device:TPU:451, one launch (start us, length us, event | category | flops | bytes accessed | tf_op | source)
XLA Modules:
  0.0 125.7 jit_solution(10909558202845865447)
XLA Ops:
  0.0 123.7 %parareal.1 = f32[1,6,2,64,256]{4,3,2,1,0:T(8,128)} custom-call(f32[1,6,2,64,256]{4,3,2,1,0:T(8,128)} %refs_0_.1, bf16[3,2,64,256]{3,2,1,0:T(8,128)(2,1)} %refs_1_.1, s32[2,64,256]{2,1,0:T(8,128)} %refs_2_.1, f32[8]{0:T(128)} %refs_3_.1, f32[8]{0:T(128)} %refs_4_.1, f32[16]{0:T(128)} %refs_5_.1, s32[16]{0:T(128)} %refs_6_.1), custom_call_target="tpu_custom_call" | custom-call | tf_op jit(solution)/shard_map/parareal/pallas_call | solution.py:518
  123.7 2.1 %copy.9 = f32[1,6,2,64,256]{4,3,2,1,0:T(8,128)} copy(f32[1,6,2,64,256]{4,3,2,1,0:T(8,128)} %parareal.1) | data formatting | bytes 1572864

commit v3 on v2

--- a/solution.py
+++ b/solution.py
@@ -195,28 +195,35 @@
 
     pl.semaphore_wait(barrier, expected)
 
-    def halo_copy(source, slot, p):
+    blocks = ny // ROWS
+
+    def halo_copy(slot, p, block):
+        start = pl.multiple_of(block * ROWS, ROWS)
+        shifted = pl.ds(start + PAD, ROWS)
+        if slot == 0:
+            source = states.at[pl.ds(0, 3), p, pl.ds(start, ROWS), :]
+        else:
+            source = disp.at[slot, :, p, shifted, :]
         return pltpu.make_async_remote_copy(
             src_ref=source,
-            dst_ref=halo.at[slot, 1 - p, :, inner, :],
-            send_sem=halo_send.at[slot, p],
-            recv_sem=halo_recv.at[slot, 1 - p],
+            dst_ref=halo.at[slot, 1 - p, :, shifted, :],
+            send_sem=halo_send.at[slot, p, block],
+            recv_sem=halo_recv.at[slot, 1 - p, block],
             device_id={"slab": slab - 1 + 2 * p},
             device_id_type=MESH,
         )
 
-    def disp_source(slot, p):
-        return disp.at[slot, :, p, inner, :]
-
-    def send_plane(source, slot, p):
+    def send_chunk(slot, p, block):
         @pl.when(has_slab[p])
         def _():
-            halo_copy(source, slot, p).start()
-
-    def await_halo(slot, side):
-        @pl.when(has_slab[side])
-        def _():
-            halo_copy(disp_source(0, 1 - side), slot, 1 - side).wait_recv()
+            halo_copy(slot, p, block).start()
+
+    def await_chunk(slot, block):
+        for side in range(2):
+
+            @pl.when(has_slab[side])
+            def _(side=side):
+                halo_copy(slot, 1 - side, block).wait_recv()
 
     def zone_copy(p):
         return pltpu.make_async_remote_copy(
@@ -250,17 +257,15 @@
         )
 
     loads[0].wait()
-    for p in range(2):
-        send_plane(states.at[pl.ds(0, 3), p], 0, p)
+    for block in range(blocks):
+        for p in range(2):
+            send_chunk(0, p, block)
     loads[1].wait()
     for p in range(2):
 
         @pl.when(has_slab[p])
         def _(p=p):
             zone_copy(p).start()
-
-    for k in range(1, windows):
-        share(states, starts, start_send, start_recv, k).start()
 
     for c in range(3):
         for p in range(2):
@@ -283,14 +288,24 @@
     amp = amp_table[cycle_index[win]]
 
     for step in range(FINE):
-        for p in range(2):
-            await_halo(step, p)
-
-            def body(block, carry, step=step, p=p):
-                start = pl.multiple_of(block * ROWS, ROWS)
-                rows = pl.ds(start, ROWS)
-                shifted = pl.ds(start + PAD, ROWS)
-                window = pl.ds(start, ROWS + 2 * PAD)
+
+        @pl.when((win + 1) // 2 == step + 1)
+        def _():
+            for k in range(1, windows):
+                share(states, starts, start_send, start_recv, k).start()
+
+        await_chunk(step, 0)
+
+        def body(block, carry, step=step):
+            @pl.when(block + 1 < blocks)
+            def _():
+                await_chunk(step, block + 1)
+
+            start = pl.multiple_of(block * ROWS, ROWS)
+            rows = pl.ds(start, ROWS)
+            shifted = pl.ds(start + PAD, ROWS)
+            window = pl.ds(start, ROWS + 2 * PAD)
+            for p in range(2):
                 low, mid, high = [], [], []
                 for c in range(3):
                     own = [disp[step, c, q, window, :] for q in range(2)]
@@ -311,14 +326,21 @@
                     else:
                         fine_end[c, p, rows, :] = placed
                         fine_end[3 + c, p, rows, :] = moved
-                return carry
-
-            lax.fori_loop(0, ny // ROWS, body, 0)
             if step + 1 < FINE:
-                send_plane(disp_source(step + 1, p), step + 1, p)
-
-    for k in range(1, windows):
-        share(fine_end, fines, fine_send, fine_recv, k).start()
+                for p in range(2):
+                    send_chunk(step + 1, p, block)
+            return carry
+
+        lax.fori_loop(0, blocks, body, 0)
+
+    def share_fine():
+        for k in range(1, windows):
+            share(fine_end, fines, fine_send, fine_recv, k).start()
+
+    @pl.when(win <= 1)
+    def _():
+        share_fine()
+
     fines[win] = fine_end[:, :, own_rows, :]
     starts[win] = states[:, :, own_rows, :]
 
@@ -396,6 +418,10 @@
                 for copy in wide_copies(n, step):
                     copy.start()
 
+        @pl.when(win == n + 1)
+        def _():
+            share_fine()
+
         for step in around:
 
             @pl.when(present(step))
@@ -474,11 +500,10 @@
 
     for n in range(windows):
 
-        @pl.when(n != win)
-        def _(n=n):
-            if n == 0:
-                shared(starts, start_recv, 0).wait_recv()
-            else:
+        if n:
+
+            @pl.when(n != win)
+            def _(n=n):
                 home(n).wait_send()
 
         @pl.when(jnp.logical_and(win != 0, n != win))
@@ -494,7 +519,11 @@
             ).wait_recv()
 
     for k in range(1, windows):
-        share(states, starts, start_send, start_recv, k).wait_send()
+
+        @pl.when(win != 0)
+        def _(k=k):
+            share(states, starts, start_send, start_recv, k).wait_send()
+
         share(fine_end, fines, fine_send, fine_recv, k).wait_send()
     for p in range(2):
 
@@ -502,7 +531,8 @@
         def _(p=p):
             zone_copy(p).wait_send()
             for slot in range(FINE):
-                halo_copy(disp_source(slot, p), slot, p).wait_send()
+                for block in range(blocks):
+                    halo_copy(slot, p, block).wait_send()
 
 
 def solution(mesh):
@@ -547,8 +577,8 @@
                 dma((7,)),
                 dma((2,)),
                 dma((2,)),
-                dma((FINE, 2)),
-                dma((FINE, 2)),
+                dma((FINE, 2, ny // ROWS)),
+                dma((FINE, 2, ny // ROWS)),
                 dma((windows,)),
                 dma((windows,)),
                 dma((windows,)),

time: 126 us -> 140 us (1.11)
  the two profiles are of different devices: /device:TPU:451 before, /device:TPU:195 now
where the time goes in v3:
time: 140 us
  Pallas kernels  137 us (98%)
  local copies, waits for them, and re-layouts  2.06 us (1%)
    pallas_call x1, Pallas kernels, shards(): pl.pallas_call(lambda *refs: kernel(windows, slabs, *refs), out_shape=jax...  137 us

profile of v3, /device:TPU:195, one launch (start us, length us, event | category | flops | bytes accessed | tf_op | source)
XLA Modules:
  0.0 139.6 jit_solution(11477889640099775499)
XLA Ops:
  0.0 137.5 %parareal.1 = f32[1,6,2,64,256]{4,3,2,1,0:T(8,128)} custom-call(f32[1,6,2,64,256]{4,3,2,1,0:T(8,128)} %refs_0_.1, bf16[3,2,64,256]{3,2,1,0:T(8,128)(2,1)} %refs_1_.1, s32[2,64,256]{2,1,0:T(8,128)} %refs_2_.1, f32[8]{0:T(128)} %refs_3_.1, f32[8]{0:T(128)} %refs_4_.1, f32[16]{0:T(128)} %refs_5_.1, s32[16]{0:T(128)} %refs_6_.1), custom_call_target="tpu_custom_call" | custom-call | tf_op jit(solution)/shard_map/parareal/pallas_call | solution.py:548
  137.5 2.1 %copy.9 = f32[1,6,2,64,256]{4,3,2,1,0:T(8,128)} copy(f32[1,6,2,64,256]{4,3,2,1,0:T(8,128)} %parareal.1) | data formatting | bytes 1572864

commit v4 on v3

--- a/solution.py
+++ b/solution.py
@@ -9,7 +9,7 @@
 DT_FINE = 0.18
 DT_COARSE = 0.36
 PAD = 8
-ROWS = 16
+ROWS = 32
 MESH = pl.DeviceIdType.MESH
 
 
@@ -337,9 +337,7 @@
         for k in range(1, windows):
             share(fine_end, fines, fine_send, fine_recv, k).start()
 
-    @pl.when(win <= 1)
-    def _():
-        share_fine()
+    share_fine()
 
     fines[win] = fine_end[:, :, own_rows, :]
     starts[win] = states[:, :, own_rows, :]
@@ -417,10 +415,6 @@
             def _(step=step):
                 for copy in wide_copies(n, step):
                     copy.start()
-
-        @pl.when(win == n + 1)
-        def _():
-            share_fine()
 
         for step in around:
 

time: 140 us -> 122 us (0.87)
  the two profiles are of different devices: /device:TPU:195 before, /device:TPU:449 now
where the time goes in v4:
time: 122 us
  Pallas kernels  120 us (98%)
  local copies, waits for them, and re-layouts  2.06 us (2%)
    pallas_call x1, Pallas kernels, shards(): pl.pallas_call(lambda *refs: kernel(windows, slabs, *refs), out_shape=jax...  120 us

profile of v4, /device:TPU:449, one launch (start us, length us, event | category | flops | bytes accessed | tf_op | source)
XLA Modules:
  0.0 121.6 jit_solution(17341736016620925819)
XLA Ops:
  0.0 119.5 %parareal.1 = f32[1,6,2,64,256]{4,3,2,1,0:T(8,128)} custom-call(f32[1,6,2,64,256]{4,3,2,1,0:T(8,128)} %refs_0_.1, bf16[3,2,64,256]{3,2,1,0:T(8,128)(2,1)} %refs_1_.1, s32[2,64,256]{2,1,0:T(8,128)} %refs_2_.1, f32[8]{0:T(128)} %refs_3_.1, f32[8]{0:T(128)} %refs_4_.1, f32[16]{0:T(128)} %refs_5_.1, s32[16]{0:T(128)} %refs_6_.1), custom_call_target="tpu_custom_call" | custom-call | tf_op jit(solution)/shard_map/parareal/pallas_call | solution.py:542
  119.6 2.1 %copy.9 = f32[1,6,2,64,256]{4,3,2,1,0:T(8,128)} copy(f32[1,6,2,64,256]{4,3,2,1,0:T(8,128)} %parareal.1) | data formatting | bytes 1572864
